TPU v7x, 512 devices: a whole 4x4x16 slice. The times are simulated.
512 devices in a mesh: tile: 128 (over x, z, core), rep: 4 (over y).
Axes of the slice: x: 4, y: 4, z: 16, core: 2. Of those that a mesh axis runs over, the one named last changes fastest.
Arguments:
- embedding: bfloat16 [2048, 64, 256], P('tile'), may hold values from -6 to 6
- prompt_tile: int32 [65536, 1], P(('tile', 'rep')), may hold values from 0 to 127; in each aligned block of 128 rows (0 to 127, 128 to 255, ...) at most 2 rows name the same one
- crop_row: int32 [65536], P(('tile', 'rep')), may hold values from 0 to 15
- crop_col: int32 [65536], P(('tile', 'rep')), may hold values from 0 to 60
- points: int32 [65536, 2], P(('tile', 'rep')), may hold values from 0 to 15
- confidence: int32 [65536], P(('tile', 'rep')), may hold values from 1 to 4
- pe_matrix: float32 [2, 128], replicated, may hold values from -5 to 5
- point_embed: float32 [256], replicated, may hold values from -5 to 5
- w_one: bfloat16 [256, 256], replicated, may hold values from -0.375 to 0.375
- w_two: bfloat16 [256, 256], replicated, may hold values from -0.375 to 0.375
- w_three: bfloat16 [256, 32], replicated, may hold values from -0.375 to 0.375
- conv_one: bfloat16 [256, 256], replicated, may hold values from -0.375 to 0.375
- conv_two: bfloat16 [64, 128], replicated, may hold values from -0.75 to 0.75
Outputs:
- mask_sum: float32 [8192, 256], P('tile')
Inputs may be any that keep to these rules, and one draw needn't show every extreme that they name: `prompt_tile`: among the prompts of one device no strip is named more than 2 times, and some device names some strip exactly 2 times.
All inputs are finite; a program needn't handle non-finite values.
Results may differ from a plain program's by a relative error of at most 0.0049.
Values may be sent and summed in bfloat16 or wider, within the bound.
No kernel may reach another device: no remote copies, remote signals or barrier semaphores. Data moves between devices by JAX's collectives and lax.ppermute only.
A program may use at most 64 MiB of HBM per device.

v0:
```python
import math

import jax
import jax.numpy as jnp
from jax import lax
from jax.sharding import PartitionSpec as P

CK = 4


def shifted(value, axis, steps):
    count = lax.axis_size(axis)
    leading, last = (max(0, -steps), min(count, count - steps))
    return lax.ppermute(value, axis, [(source, source + steps) for source in range(leading, last)])


def prompt_heads(points, pe_matrix, point_embed, w_one, w_two, w_three):
    coords = (points.astype(jnp.float32) + 0.5) / (4.0 * CK) * 2.0 - 1.0
    angles = (coords[:, 0:1] * pe_matrix[0][None, :] + coords[:, 1:2] * pe_matrix[1][None, :]) * (
        2.0 * math.pi
    )
    tokens = (
        jnp.concatenate([jnp.sin(angles), jnp.cos(angles)], axis=1) + point_embed[None, :]
    ).astype(jnp.bfloat16)
    hidden_one = jax.nn.relu(jnp.dot(tokens, w_one, preferred_element_type=jnp.float32)).astype(
        jnp.bfloat16
    )
    hidden_two = jax.nn.relu(jnp.dot(hidden_one, w_two, preferred_element_type=jnp.float32)).astype(
        jnp.bfloat16
    )
    return jnp.dot(hidden_two, w_three, preferred_element_type=jnp.float32).astype(jnp.bfloat16)


def mask_terms(crop_cells, head_rows, scale_rows, conv_one, conv_two):
    amount, crop_side, channels = (crop_cells.shape[0], crop_cells.shape[1], crop_cells.shape[3])
    mid_width = conv_one.shape[1] // 4
    narrow = conv_two.shape[1] // 4
    first_up = jnp.dot(
        crop_cells.reshape(amount * crop_side * crop_side, channels),
        conv_one,
        preferred_element_type=jnp.float32,
    )
    first_up = first_up.reshape(amount * crop_side * crop_side * 4, mid_width)
    centre = first_up - jnp.mean(first_up, axis=1, keepdims=True)
    normed = centre * lax.rsqrt(jnp.mean(centre * centre, axis=1, keepdims=True) + 1e-06)
    active = jax.nn.gelu(normed, approximate=False).astype(jnp.bfloat16)
    second = jnp.dot(active, conv_two, preferred_element_type=jnp.float32)
    upscaled = (
        jax.nn.gelu(second, approximate=False)
        .astype(jnp.bfloat16)
        .reshape(amount, crop_side * crop_side * 16, narrow)
    )
    logits = jnp.einsum("nqc,nc->nq", upscaled, head_rows, preferred_element_type=jnp.float32)
    logits = logits.reshape(amount, crop_side, crop_side, 2, 2, 2, 2).transpose(0, 1, 3, 5, 2, 4, 6)
    logits = logits.reshape(amount, 4 * crop_side, 4 * crop_side)
    return (logits * scale_rows[:, None, None]).astype(jnp.bfloat16)


def terms_in_blocks(crop_cells, head_rows, scale_rows, conv_one, conv_two):
    amount = crop_cells.shape[0]
    block_size = 64
    groups = amount // block_size

    def one_block(group_in):
        return mask_terms(group_in[0], group_in[1], group_in[2], conv_one, conv_two)

    result = lax.map(
        one_block,
        (
            crop_cells.reshape((groups, block_size) + crop_cells.shape[1:]),
            head_rows.reshape(groups, block_size, head_rows.shape[1]),
            scale_rows.reshape(groups, block_size),
        ),
    )
    return result.reshape((amount,) + result.shape[2:])


def cut_crops(extended, row_starts, col_starts):
    height, width, channels = (extended.shape[0], extended.shape[1], extended.shape[2])
    offsets = jnp.arange(CK, dtype=jnp.int32)
    cell_rows = row_starts.astype(jnp.int32)[:, None, None] + offsets[None, :, None]
    cell_cols = col_starts.astype(jnp.int32)[:, None, None] + offsets[None, None, :]
    cell_index = (cell_rows * width + cell_cols).reshape(-1)
    picked = jnp.take(extended.reshape(height * width, channels), cell_index, axis=0)
    return picked.reshape(row_starts.shape[0], CK, CK, channels)


def place_patches(patches, row_starts, col_starts, height, breadth):
    amount, patch_side = (patches.shape[0], patches.shape[1])
    block_size = 64
    groups = amount // block_size
    offsets = jnp.arange(patch_side, dtype=jnp.int32)
    canvas_rows = jnp.arange(height, dtype=jnp.int32)
    canvas_cols = jnp.arange(breadth, dtype=jnp.int32)

    def add_block(canvas, block_in):
        patch_in, row_at, col_at = block_in
        col_table = (
            4 * col_at[:, None, None] + offsets[None, :, None] == canvas_cols[None, None, :]
        ).astype(jnp.bfloat16)
        placed = jnp.einsum(
            "byx,bxs->bys", patch_in, col_table, preferred_element_type=jnp.float32
        ).astype(jnp.bfloat16)
        row_table = (
            4 * row_at[:, None, None] + offsets[None, :, None] == canvas_rows[None, None, :]
        ).astype(jnp.bfloat16)
        added = jnp.einsum(
            "kr,ks->rs",
            row_table.reshape(block_size * patch_side, height),
            placed.reshape(block_size * patch_side, breadth),
            preferred_element_type=jnp.float32,
        )
        return (canvas + added, None)

    canvas, unused = lax.scan(
        add_block,
        jnp.zeros((height, breadth), jnp.float32),
        (
            patches.reshape(groups, block_size, patch_side, patch_side),
            row_starts.reshape(groups, block_size),
            col_starts.reshape(groups, block_size),
        ),
    )
    return canvas


def on_device(
    embedding,
    prompt_tile,
    crop_row,
    crop_col,
    points,
    confidence,
    pe_matrix,
    point_embed,
    w_one,
    w_two,
    w_three,
    conv_one,
    conv_two,
):
    tile_count = lax.axis_size("tile")
    strip_height = embedding.shape[0]
    breadth = 4 * embedding.shape[1]
    prompt_count = prompt_tile.shape[0]
    slot_most = max(2, 2 * prompt_count // tile_count)
    slot_total = tile_count * slot_most
    dynamic_heads = prompt_heads(points, pe_matrix, point_embed, w_one, w_two, w_three)
    head_width = dynamic_heads.shape[1]
    target = prompt_tile[:, 0]
    onehot = (target[:, None] == jnp.arange(tile_count, dtype=jnp.int32)[None, :]).astype(jnp.int32)
    earlier = jnp.cumsum(onehot, axis=0) - onehot
    rank_in = jnp.sum(earlier * onehot, axis=1)
    slot_index = target * slot_most + rank_in
    request = jnp.stack([crop_row, crop_col, confidence], axis=1)
    request_slots = (
        jnp.zeros((slot_total, 3), jnp.int32)
        .at[slot_index]
        .set(request)
        .reshape(tile_count, slot_most, 3)
    )
    rows_below = shifted(embedding[: CK - 1], "tile", -1)
    extended = jnp.concatenate([embedding, rows_below], axis=0)
    head_slots = jnp.zeros((slot_total, head_width), jnp.bfloat16).at[slot_index].set(dynamic_heads)
    head_slots = head_slots.reshape(tile_count, slot_most, head_width)
    head_in = lax.all_to_all(head_slots, "tile", split_axis=0, concat_axis=0, tiled=True)
    request_in = lax.all_to_all(request_slots, "tile", split_axis=0, concat_axis=0, tiled=True)
    sources = request_in.shape[0]
    per_source = request_in.shape[1]
    flat_request = request_in.reshape(sources * per_source, 3)
    crop_cells = cut_crops(extended, flat_request[:, 0], flat_request[:, 1])
    patches = terms_in_blocks(
        crop_cells,
        head_in.reshape(sources * per_source, head_width),
        flat_request[:, 2].astype(jnp.float32) / 4.0,
        conv_one,
        conv_two,
    )
    patch_slots = patches.reshape(sources, per_source, 4 * CK, 4 * CK)
    owner_flat = request_in.reshape(slot_total, 3)
    canvas = place_patches(
        patch_slots.reshape(slot_total, 4 * CK, 4 * CK),
        owner_flat[:, 0],
        owner_flat[:, 1],
        4 * strip_height + 4 * CK - 4,
        breadth,
    )
    summed = lax.psum(canvas, "rep")
    spilled = shifted(summed[4 * strip_height :], "tile", 1)
    return summed[: 4 * strip_height] + jnp.pad(
        spilled, ((0, 4 * strip_height - spilled.shape[0]), (0, 0))
    )


def solution(mesh):
    return jax.shard_map(
        on_device,
        mesh=mesh,
        in_specs=(
            P("tile", None, None),
            P(("tile", "rep"), None),
            P(("tile", "rep")),
            P(("tile", "rep")),
            P(("tile", "rep"), None),
            P(("tile", "rep")),
            P(),
            P(),
            P(),
            P(),
            P(),
            P(),
            P(),
        ),
        out_specs=P("tile", None),
        check_vma=False,
    )
```

profile of v0, /device:TPU:1, one launch (start us, length us, event | category | flops | bytes accessed | tf_op | source)
XLA Modules:
  0.0 255.6 jit_solution(17116012527974906901)
XLA Ops:
  9.8 1.5 scatter_custom_fusion
  11.3 20.4 %all-to-all-start = ((s32[128,2,3]{2,1,0:T(2,128)}), s32[128,2,3]{2,1,0:T(2,128)S(1)}, u32[]{:S(2)}, u32[]{:S(2)}) async-start(s32[128,2,3]{2,1,0:T(2,128)} %bitcast.13), calls=%async_computation | async-start | bytes 262144 | tf_op jit(solution)/shard_map/all_to_all | solution.py:167
  32.6 2.8 %collective-permute-start = (bf16[3,64,256]{2,1,0:T(8,128)(2,1)S(1)}, bf16[3,64,256]{2,1,0:T(8,128)(2,1)S(1)}, u32[]{:S(2)}, u32[]{:S(2)}) collective-permute-start(bf16[3,64,256]{2,1,0:T(8,128)(2,1)S(1)} %slice.36), channel_id=1, source_target_pairs={{4,0},{8,4},{12,8},{16,12},{20,16},{24,20},{28,24},{32,28},{36,32}... | collective-permute-start | bytes 294920 | tf_op jit(solution)/shard_map/ppermute | solution.py:14
  37.2 1.2 fusion.74
  39.5 1.5 scatter_custom_fusion.1
  40.9 8.0 %all-to-all-done = s32[128,2,3]{2,1,0:T(2,128)S(1)} async-done(((s32[128,2,3]{2,1,0:T(2,128)}), s32[128,2,3]{2,1,0:T(2,128)S(1)}, u32[]{:S(2)}, u32[]{:S(2)}) %all-to-all-start) | async-done | bytes 3104 | tf_op jit(solution)/shard_map/all_to_all | solution.py:167
  49.0 8.0 %all-to-all-start.1 = ((bf16[128,2,32]{2,1,0:T(2,128)(2,1)}), bf16[128,2,32]{2,1,0:T(2,128)(2,1)}, u32[]{:S(2)}, u32[]{:S(2)}) async-start(bf16[128,2,32]{2,1,0:T(2,128)(2,1)} %bitcast.23), calls=%async_computation.1 | async-start | bytes 131072 | tf_op jit(solution)/shard_map/all_to_all | solution.py:166
  60.1 14.6 %gather_fusion = bf16[4096,256]{1,0:T(8,128)(2,1)S(1)} fusion(bf16[1216,256]{1,0:T(8,128)(2,1)S(1)} %bitcast.78, s32[4096]{0:T(1024)S(1)} %broadcast_clamp_fusion), kind=kCustom, calls=%fused_computation | custom fusion | bytes 4210688 | tf_op jit(solution)/shard_map/jit(_take)/gather | solution.py:84
  74.7 2.1 gather.7
  76.8 3.4 %broadcast_select_fusion = bf16[4,64,4,4,256]{4,3,2,1,0:T(4,128)(2,1)S(1)} fusion(bf16[4,64,4,4,256]{4,3,2,1,0:T(4,128)(2,1)} %gather.7, pred[4,64,4,4]{3,2,1,0:T(4,128)(4,1)S(1)} %copy.42), kind=kLoop, calls=%fused_computation.104 | loop fusion | flops 1048576 | bytes 4198400 | tf_op jit(solution)/shard_map/jit(_take)/select_n | solution.py:84
  80.3 92.5 %while.22 = (s32[]{:T(128)}, bf16[4,64,16,16]{1,3,2,0:T(8,128)(2,1)}, bf16[4,64,4,4,256]{4,3,2,1,0:T(4,128)(2,1)S(1)}, bf16[256,256]{1,0:T(8,128)(2,1)S(1)}, bf1...) while((s32[]{:T(128)}, ...), condition=%wide.region_7.8_spmd, body=%wide.region_4.7_spmd.sunk | while | flops 255102976 | bytes 30717376 | solution.py:67
  82.9 1.3 multiply_reduce_fusion.3
  84.2 10.8 %fusion.126 = bf16[4096,128]{1,0:T(8,128)(2,1)S(1)} fusion(bf16[64,128]{1,0:T(8,128)(2,1)S(1)} %copy-done.9, f32[4096,64]{1,0:T(8,128)S(1)} %reshape.309, f32[4096]{0:T(1024)S(1)} %add_rsqrt_fusion.2, f32[4096]{0:T(1024)S(1)} %broadcast_multiply_fusion.2), kind=kOutput, calls=%fused_computation.13.clone.1 | convolution fusion | flops 118751232 | bytes 2146304 | tf_op jit(solution)/shard_map/while/body/eval_jaxpr/dot_general | solution.py:47
  95.0 3.3 %reshape.310 = bf16[64,256,32]{2,1,0:T(8,128)(2,1)} reshape(bf16[4096,128]{1,0:T(8,128)(2,1)S(1)} %fusion.126) | data formatting | bytes 2097152 | tf_op jit(solution)/shard_map/while/body/eval_jaxpr/reshape | solution.py:51
  99.0 3.5 %fusion.127 = f32[64,1,256]{2,1,0:T(1,128)S(1)} fusion(bf16[64,256,32]{2,1,0:T(8,128)(2,1)} %reshape.310, bf16[64,32,1]{1,0,2:T(8,128)(2,1)S(1)} %dynamic-slice_bitcast_fusion.2), kind=kOutput, calls=%fused_computation.48.clone.1 | convolution fusion | flops 1048576 | bytes 1118208 | tf_op jit(solution)/shard_map/while/body/eval_jaxpr/nqc,nc->nq/dot_general | solution.py:53
  106.0 1.3 multiply_reduce_fusion.3
  107.3 10.8 %fusion.126 = bf16[4096,128]{1,0:T(8,128)(2,1)S(1)} fusion(bf16[64,128]{1,0:T(8,128)(2,1)S(1)} %copy-done.9, f32[4096,64]{1,0:T(8,128)S(1)} %reshape.309, f32[4096]{0:T(1024)S(1)} %add_rsqrt_fusion.2, f32[4096]{0:T(1024)S(1)} %broadcast_multiply_fusion.2), kind=kOutput, calls=%fused_computation.13.clone.1 | convolution fusion | flops 118751232 | bytes 2146304 | tf_op jit(solution)/shard_map/while/body/eval_jaxpr/dot_general | solution.py:47
  118.2 3.3 %reshape.310 = bf16[64,256,32]{2,1,0:T(8,128)(2,1)} reshape(bf16[4096,128]{1,0:T(8,128)(2,1)S(1)} %fusion.126) | data formatting | bytes 2097152 | tf_op jit(solution)/shard_map/while/body/eval_jaxpr/reshape | solution.py:51
  122.2 3.5 %fusion.127 = f32[64,1,256]{2,1,0:T(1,128)S(1)} fusion(bf16[64,256,32]{2,1,0:T(8,128)(2,1)} %reshape.310, bf16[64,32,1]{1,0,2:T(8,128)(2,1)S(1)} %dynamic-slice_bitcast_fusion.2), kind=kOutput, calls=%fused_computation.48.clone.1 | convolution fusion | flops 1048576 | bytes 1118208 | tf_op jit(solution)/shard_map/while/body/eval_jaxpr/nqc,nc->nq/dot_general | solution.py:53
  129.1 1.3 multiply_reduce_fusion.3
  130.4 10.8 %fusion.126 = bf16[4096,128]{1,0:T(8,128)(2,1)S(1)} fusion(bf16[64,128]{1,0:T(8,128)(2,1)S(1)} %copy-done.9, f32[4096,64]{1,0:T(8,128)S(1)} %reshape.309, f32[4096]{0:T(1024)S(1)} %add_rsqrt_fusion.2, f32[4096]{0:T(1024)S(1)} %broadcast_multiply_fusion.2), kind=kOutput, calls=%fused_computation.13.clone.1 | convolution fusion | flops 118751232 | bytes 2146304 | tf_op jit(solution)/shard_map/while/body/eval_jaxpr/dot_general | solution.py:47
  141.3 3.3 %reshape.310 = bf16[64,256,32]{2,1,0:T(8,128)(2,1)} reshape(bf16[4096,128]{1,0:T(8,128)(2,1)S(1)} %fusion.126) | data formatting | bytes 2097152 | tf_op jit(solution)/shard_map/while/body/eval_jaxpr/reshape | solution.py:51
  145.3 3.5 %fusion.127 = f32[64,1,256]{2,1,0:T(1,128)S(1)} fusion(bf16[64,256,32]{2,1,0:T(8,128)(2,1)} %reshape.310, bf16[64,32,1]{1,0,2:T(8,128)(2,1)S(1)} %dynamic-slice_bitcast_fusion.2), kind=kOutput, calls=%fused_computation.48.clone.1 | convolution fusion | flops 1048576 | bytes 1118208 | tf_op jit(solution)/shard_map/while/body/eval_jaxpr/nqc,nc->nq/dot_general | solution.py:53
  150.0 1.0 copy-done.1
  152.2 1.3 multiply_reduce_fusion.3
  153.6 10.8 %fusion.126 = bf16[4096,128]{1,0:T(8,128)(2,1)S(1)} fusion(bf16[64,128]{1,0:T(8,128)(2,1)S(1)} %copy-done.9, f32[4096,64]{1,0:T(8,128)S(1)} %reshape.309, f32[4096]{0:T(1024)S(1)} %add_rsqrt_fusion.2, f32[4096]{0:T(1024)S(1)} %broadcast_multiply_fusion.2), kind=kOutput, calls=%fused_computation.13.clone.1 | convolution fusion | flops 118751232 | bytes 2146304 | tf_op jit(solution)/shard_map/while/body/eval_jaxpr/dot_general | solution.py:47
  164.4 3.3 %reshape.310 = bf16[64,256,32]{2,1,0:T(8,128)(2,1)} reshape(bf16[4096,128]{1,0:T(8,128)(2,1)S(1)} %fusion.126) | data formatting | bytes 2097152 | tf_op jit(solution)/shard_map/while/body/eval_jaxpr/reshape | solution.py:51
  168.4 3.5 %fusion.127 = f32[64,1,256]{2,1,0:T(1,128)S(1)} fusion(bf16[64,256,32]{2,1,0:T(8,128)(2,1)} %reshape.310, bf16[64,32,1]{1,0,2:T(8,128)(2,1)S(1)} %dynamic-slice_bitcast_fusion.2), kind=kOutput, calls=%fused_computation.48.clone.1 | convolution fusion | flops 1048576 | bytes 1118208 | tf_op jit(solution)/shard_map/while/body/eval_jaxpr/nqc,nc->nq/dot_general | solution.py:53
  172.8 11.3 %while.23 = (s32[]{:T(128)}, f32[76,256]{1,0:T(8,128)S(1)}, s32[4,64]{1,0:T(4,128)}, bf16[4,64,16,16]{1,3,2,0:T(8,128)(2,1)}, s32[4,64]{1,0:T(4,128)}, /*index=5*/s32[]{:T(128)}, s32[]{:T(128)}) while((s32[]{:T(128)}, f32[76,256]{1,0:T(8,128)S(1)}, s32[4,64]{1,0:T(4,128)}, bf16[4,64,16,16]{1,3,2,0:T(8,128)(2,1)}, ...), condition=%wide.region_9.10_spmd.clone.clone, body=%wide.region_8.9_spmd.clone.clone.sunk | while | flops 48877696 | bytes 1394271 | solution.py:115
  184.7 55.5 %all-reduce.3.cloned.1.call-done = f32[76,256]{1,0:T(8,128)} async-done(((f32[76,256]{1,0:T(8,128)}), f32[76,256]{1,0:T(8,128)}) %all-reduce.3.cloned.1.call-update) | async-done | bytes 77840 | tf_op jit(solution)/shard_map/psum | solution.py:188
  240.9 5.5 %collective-permute-start.1 = (f32[12,256]{1,0:T(8,128)S(1)}, f32[12,256]{1,0:T(8,128)S(1)}, u32[]{:S(2)}, u32[]{:S(2)}) collective-permute-start(f32[12,256]{1,0:T(8,128)S(1)} %slice.51), channel_id=1, source_target_pairs={{0,4},{4,8},{8,12},{12,16},{16,20},{20,24},{24,28},{28,32},{32,36}... | collective-permute-start | bytes 36872 | tf_op jit(solution)/shard_map/ppermute | solution.py:14
  247.3 1.5 slice_add_fusion
  (155 shorter events, 38.8 us)
Async XLA Ops:
  6.5 30.7 %copy-start = (bf16[256,256]{1,0:T(8,128)(2,1)S(1)}, bf16[256,256]{1,0:T(8,128)(2,1)}, u32[]{:S(2)}) copy-start(bf16[256,256]{1,0:T(8,128)(2,1)} %param.26) | copy-start | bytes 393220
  11.3 37.7 %all-to-all-start = ((s32[128,2,3]{2,1,0:T(2,128)}), s32[128,2,3]{2,1,0:T(2,128)S(1)}, u32[]{:S(2)}, u32[]{:S(2)}) async-start(s32[128,2,3]{2,1,0:T(2,128)} %bitcast.13), calls=%async_computation | async-start | bytes 262144 | tf_op jit(solution)/shard_map/all_to_all | solution.py:167
  31.7 28.3 %copy-start.4 = (bf16[16,64,256]{2,1,0:T(8,128)(2,1)S(1)}, bf16[16,64,256]{2,1,0:T(8,128)(2,1)}, u32[]{:S(2)}) copy-start(bf16[16,64,256]{2,1,0:T(8,128)(2,1)} %param.17) | copy-start | bytes 1572868
  32.6 27.4 %collective-permute-start = (bf16[3,64,256]{2,1,0:T(8,128)(2,1)S(1)}, bf16[3,64,256]{2,1,0:T(8,128)(2,1)S(1)}, u32[]{:S(2)}, u32[]{:S(2)}) collective-permute-start(bf16[3,64,256]{2,1,0:T(8,128)(2,1)S(1)} %slice.36), channel_id=1, source_target_pairs={{4,0},{8,4},{12,8},{16,12},{20,16},{24,20},{28,24},{32,28},{36,32}... | collective-permute-start | bytes 294920 | tf_op jit(solution)/shard_map/ppermute | solution.py:14
  49.0 31.3 %all-to-all-start.1 = ((bf16[128,2,32]{2,1,0:T(2,128)(2,1)}), bf16[128,2,32]{2,1,0:T(2,128)(2,1)}, u32[]{:S(2)}, u32[]{:S(2)}) async-start(bf16[128,2,32]{2,1,0:T(2,128)(2,1)} %bitcast.23), calls=%async_computation.1 | async-start | bytes 131072 | tf_op jit(solution)/shard_map/all_to_all | solution.py:166
  57.0 183.2 %all-reduce.3.cloned.1.call-start = ((), (), s32[]{:S(2)}) async-start(), calls=%async_computation.2 | async-start | bytes 163840 | tf_op jit(solution)/shard_map/psum | solution.py:188
  57.6 0.6 copy-start.7
  57.6 0.6 copy-start.8
  76.8 3.4 %copy-start.3 = (bf16[256,256]{1,0:T(8,128)(2,1)S(1)}, bf16[256,256]{1,0:T(8,128)(2,1)}, u32[]{:S(2)}) copy-start(bf16[256,256]{1,0:T(8,128)(2,1)} %param.28) | copy-start | bytes 393220
  80.2 92.5 %copy-start.5 = (f32[76,256]{1,0:T(8,128)S(1)}, f32[76,256]{1,0:T(8,128)}, u32[]{:S(2)}) copy-start(f32[76,256]{1,0:T(8,128)} %custom-call) | copy-start | bytes 233476
  80.3 1.3 copy-start.1
  82.2 1.9 copy-start.9
  99.0 4.3 %copy-start.2 = (bf16[4,64,4,4,256]{4,3,2,1,0:T(4,128)(2,1)S(1)}, bf16[4,64,4,4,256]{4,3,2,1,0:T(4,128)(2,1)}, u32[]{:S(2)}) copy-start(bf16[4,64,4,4,256]{4,3,2,1,0:T(4,128)(2,1)} %copy-done.1) | copy-start | bytes 6291460 | tf_op jit(solution)/shard_map/while
  103.4 1.3 copy-start.1
  105.3 1.9 copy-start.9
  122.2 4.4 %copy-start.2 = (bf16[4,64,4,4,256]{4,3,2,1,0:T(4,128)(2,1)S(1)}, bf16[4,64,4,4,256]{4,3,2,1,0:T(4,128)(2,1)}, u32[]{:S(2)}) copy-start(bf16[4,64,4,4,256]{4,3,2,1,0:T(4,128)(2,1)} %copy-done.1) | copy-start | bytes 6291460 | tf_op jit(solution)/shard_map/while
  126.5 1.3 copy-start.1
  128.5 1.9 copy-start.9
  145.3 4.4 %copy-start.2 = (bf16[4,64,4,4,256]{4,3,2,1,0:T(4,128)(2,1)S(1)}, bf16[4,64,4,4,256]{4,3,2,1,0:T(4,128)(2,1)}, u32[]{:S(2)}) copy-start(bf16[4,64,4,4,256]{4,3,2,1,0:T(4,128)(2,1)} %copy-done.1) | copy-start | bytes 6291460 | tf_op jit(solution)/shard_map/while
  149.6 1.3 copy-start.1
  151.6 1.9 copy-start.9
  168.4 4.4 %copy-start.2 = (bf16[4,64,4,4,256]{4,3,2,1,0:T(4,128)(2,1)S(1)}, bf16[4,64,4,4,256]{4,3,2,1,0:T(4,128)(2,1)}, u32[]{:S(2)}) copy-start(bf16[4,64,4,4,256]{4,3,2,1,0:T(4,128)(2,1)} %copy-done.1) | copy-start | bytes 6291460 | tf_op jit(solution)/shard_map/while
  184.1 0.6 copy-start.6
  240.9 6.4 %collective-permute-start.1 = (f32[12,256]{1,0:T(8,128)S(1)}, f32[12,256]{1,0:T(8,128)S(1)}, u32[]{:S(2)}, u32[]{:S(2)}) collective-permute-start(f32[12,256]{1,0:T(8,128)S(1)} %slice.51), channel_id=1, source_target_pairs={{0,4},{4,8},{8,12},{12,16},{16,20},{20,24},{24,28},{28,32},{32,36}... | collective-permute-start | bytes 36872 | tf_op jit(solution)/shard_map/ppermute | solution.py:14
Sparse Core Ops, SparseCore 0:
  184.9 55.3 all-reduce.2
where the time goes:
time: 258 us; the launch traced here: 256 us
  waiting for transfers between devices  64.4 us (25%)
  matrix products  64.2 us (25%)
  local copies, waits for them, and re-layouts  53.2 us (21%)
  starting transfers between devices  36.9 us (14%)
  other arithmetic  22.7 us (9%)
  between operations  13.6 us (5%)
    psum x1, waiting for transfers between devices, on_device(): summed = lax.psum(canvas, 'rep')  55.5 us
    dot_general x4, matrix products, mask_terms(): second = jnp.dot(active, conv_two, preferred_element_type=jnp.float32)  43.4 us
    all_to_all x1, starting transfers between devices, on_device(): lax.all_to_all(request_slots, 'tile', split_axis=0, concat_axis=0, tiled=...  20.4 us
    gather x2, local copies, waits for them, and re-layouts, cut_crops(): jnp.take(extended.reshape(height * width, channels), cell_index, axis=0)  16.7 us
    dot_general x4, matrix products, mask_terms(): jnp.einsum('nqc,nc->nq', upscaled, head_rows, preferred_element_type=jnp....  14 us
    reshape x4, local copies, waits for them, and re-layouts, mask_terms(): upscaled = jax.nn.gelu(second, approximate=False).astype(jnp.bfloat16).re...  13.1 us
    ppermute x2, starting transfers between devices, shifted(): lax.ppermute(value, axis, [(source, source + steps) for source in range(l...  8.33 us
    all_to_all x1, waiting for transfers between devices, on_device(): lax.all_to_all(request_slots, 'tile', split_axis=0, concat_axis=0, tiled=...  8.04 us
  transfers between devices with their start and end apart: 5, of which 3 were waited for; matrix products, arithmetic and copies ran while one was open for 11% of the time, Pallas kernels for 0%

commit v1 on v0

v1 whole, which is shorter than its diff:
```python
import math

import jax
import jax.numpy as jnp
from jax import lax
from jax.experimental import pallas as pl
from jax.experimental.pallas import tpu as pltpu
from jax.sharding import Mesh
from jax.sharding import PartitionSpec as P

CK = 4
C = 256
C1 = 64
C2 = 32
ROWS_T = 16
EW = 64
P_DEV = 128
NX, NZ, NC, NR = 4, 16, 2, 4
CELLS = ROWS_T * EW
F32 = jnp.float32
BF16 = jnp.bfloat16
I32 = jnp.int32


def iota(shape, dim):
    return lax.broadcasted_iota(I32, shape, dim)


def nt(a, b):
    return lax.dot_general(a, b, (((1,), (1,)), ((), ())), preferred_element_type=F32)


def nn(a, b):
    return jnp.dot(a, b, preferred_element_type=F32)


def gelu(v):
    return 0.5 * v * (1.0 + lax.erf(v * (1.0 / math.sqrt(2.0))))


def local_tables(emb, one, two, pe, bias, w1, w2, w3, up_ref, head_ref):
    q = iota((256, P_DEV), 0)
    first = ((q >> 4).astype(F32) + 0.5) / (4.0 * CK) * 2.0 - 1.0
    second = ((q & 15).astype(F32) + 0.5) / (4.0 * CK) * 2.0 - 1.0
    pe_value = pe[...]
    angles = (first * pe_value[0:1, :] + second * pe_value[1:2, :]) * (2.0 * math.pi)
    tokens = (jnp.concatenate([jnp.sin(angles), jnp.cos(angles)], axis=1) + bias[...]).astype(BF16)
    hidden = jnp.maximum(nn(tokens, w1[...]), 0.0).astype(BF16)
    hidden = jnp.maximum(nn(hidden, w2[...]), 0.0).astype(BF16)
    head_ref[...] = nn(hidden, w3[...]).astype(BF16)

    row = iota((512, P_DEV), 0)
    k, x, y = row >> 4, (row >> 2) & 3, row & 3
    pick = (iota((512, P_DEV), 1) == (2 * (y & 1) + (x & 1)) * C2 + k).astype(BF16)
    row = iota((512, 256), 0)
    off = 2 * ((row & 3) >> 1) + (((row >> 2) & 3) >> 1)
    keep = (iota((512, 256), 1) >> 6) == off
    two_tiled = jnp.concatenate([two[...]] * 4, axis=0)
    wide = jnp.where(keep, nt(pick, two_tiled), 0.0).astype(BF16)
    one_t = one[...].astype(F32).T.astype(BF16)

    def block(i, carry):
        start = pl.multiple_of(i * 128, 128)
        first_up = nt(one_t, emb[pl.ds(start, 128), :])
        parts = []
        for o in range(4):
            v = first_up[o * C1 : (o + 1) * C1, :]
            v = v - jnp.mean(v, axis=0, keepdims=True)
            v = v * lax.rsqrt(jnp.mean(v * v, axis=0, keepdims=True) + 1e-06)
            parts.append(gelu(v).astype(BF16))
        active = jnp.concatenate(parts, axis=0)
        up_ref[:, pl.ds(start, 128)] = gelu(nn(wide, active)).astype(BF16)
        return carry

    lax.fori_loop(0, CELLS // 128, block, 0)


def gathered_in(refs, bufs, sems):
    copies = [pltpu.make_async_copy(r, b, sems.at[i]) for i, (r, b) in enumerate(zip(refs, bufs))]
    for c in copies:
        c.start()
    for c in copies:
        c.wait()


def store_out(up_buf, head_buf, up_ref, head_ref, sems):
    copies = [
        pltpu.make_async_copy(up_buf, up_ref, sems.at[0]),
        pltpu.make_async_copy(head_buf, head_ref, sems.at[1]),
    ]
    for c in copies:
        c.start()
    for c in copies:
        c.wait()


def is_early():
    z = lax.axis_index("z")
    return (z <= 4) | (z >= 12)


def slots_kernel(early, tile, row, col, pts, conf, *rest):
    weights, (send, up, head), scratch = rest[:8], rest[8:11], rest[11:]
    bufs, (up_buf, head_buf, sems) = scratch[:8], scratch[8:]
    t = tile[...]
    names = (iota((P_DEV, P_DEV), 0) == t).astype(F32)
    before = (iota((P_DEV, P_DEV), 0) < iota((P_DEV, P_DEV), 1)).astype(BF16)
    count = nn(names.astype(BF16), before)
    rank = jnp.sum(names * count, axis=0, keepdims=True).astype(I32)
    values = [row[...], col[...], conf[...], pts[0:1, :], pts[1:2, :]]
    group = iota((16, P_DEV), 0)
    x_of, s_of = group >> 2, group & 3
    dest = iota((NZ * NC, P_DEV), 0)

    def part(target, rank_at, values):
        mask = ((target >> 5) == x_of) & (rank_at == s_of)
        rows = [jnp.where(mask, v.astype(F32), 0.0) for v in values]
        rows += [jnp.zeros((16, P_DEV), F32)] * 3
        return nt(
            ((target & 31) == dest).astype(BF16), jnp.concatenate(rows, axis=0).astype(BF16)
        )

    out = part(t, rank, values) + part(t + 1, rank + 2, [values[0] - ROWS_T] + values[1:])
    send[...] = out.reshape(NZ * NC, 1, 128)

    @pl.when(early[0] == 1)
    def _():
        gathered_in(weights, bufs, sems)
        local_tables(*bufs, up_buf, head_buf)
        store_out(up_buf, head_buf, up, head, sems)


def late_kernel(early, up_in, head_in, *rest):
    weights, (up, head), scratch = rest[:8], rest[8:10], rest[10:]
    bufs, (up_buf, head_buf, sems) = scratch[:8], scratch[8:]

    @pl.when(early[0] != 1)
    def _():
        gathered_in(weights, bufs, sems)
        local_tables(*bufs, up_buf, head_buf)
        store_out(up_buf, head_buf, up, head, sems)


def regroup_kernel(got, send):
    r = got[...].reshape(NZ * NC, 128)
    r = jnp.concatenate([r] * 4, axis=0)
    keep = (iota((128, 128), 1) & 3) == (iota((128, 128), 0) >> 5)
    r = jnp.where(keep, r, 0.0).astype(BF16)
    at, lane = iota((32, 128), 0), iota((32, 128), 1)
    pick = ((lane >> 4) == (at & 7)) & (((lane >> 2) & 3) == (at >> 3))
    out = nt(pick.astype(BF16), r)
    for x in range(NX):
        for y in range(NR):
            send[x * NR + y] = out[x * 8 : (x + 1) * 8, :].astype(BF16)


def mask_kernel(got, up, head, out):
    lane = iota((8, 128), 1)
    own, below = [], []
    for j in range(8):
        a, b = got[j].astype(F32), got[j + 8].astype(F32)
        own.append(jnp.where(lane < 64, a, pltpu.roll(b, 64, 1)))
        below.append(jnp.where(lane < 64, pltpu.roll(a, 64, 1), b))
    own, below = jnp.concatenate(own, axis=1), jnp.concatenate(below, axis=1)
    many = 1024
    r_at = iota((16, many), 0).astype(F32)
    c_at = iota((EW, many), 0).astype(F32)
    table = head[...]

    def one_hot(v, at):
        return (at == v).astype(BF16)

    def factors(v, rows):
        row, col, conf, first, second = (v[i : i + 1, :] for i in range(5))
        hot_a, hot_b = one_hot(first, r_at), one_hot(second, r_at)
        hot = jnp.concatenate([hot_a[i : i + 1, :] * hot_b for i in range(16)], axis=0)
        heads = lax.dot_general(table, hot, (((0,), (0,)), ((), ())), preferred_element_type=F32)
        heads = heads.astype(BF16)
        d = r_at - row
        in_row = ((d >= 0.0) & (d <= 3.0)).astype(BF16)
        d = c_at - col
        in_col = jnp.where((d >= 0.0) & (d <= 3.0), conf, 0.0).astype(BF16)
        blank = jnp.zeros((EW, many), BF16)
        even, odd = jnp.concatenate([in_col, blank], axis=0), jnp.concatenate([blank, in_col], axis=0)
        lefts = [heads * in_row[i : i + 1, :] for i in range(rows)]
        return (
            nt(jnp.concatenate(lefts[0::2], axis=0), even)
            + nt(jnp.concatenate(lefts[1::2], axis=0), odd)
        )

    total = factors(own, 16)
    spill = factors(below, 4)
    total = jnp.concatenate([total[:64] + spill, total[64:]], axis=0)

    sub = iota((8, 128), 0)
    mine = (sub >> 2) == (iota((8, 128), 1) >> 6)
    blocks = []
    for j in range(8):
        h = total[j * 32 : (j + 1) * 32, :]
        low, high = jnp.zeros((8, 128), F32), jnp.zeros((8, 128), F32)
        for k in range(C2):
            u = up[k * 16 : (k + 1) * 16, j * 128 : (j + 1) * 128].astype(F32)
            w = h[k : k + 1, :]
            low, high = low + u[:8] * w, high + u[8:] * w
        pieces = []
        for v in (low, high):
            turned = pltpu.roll(v, 4, 0)
            pieces.append(jnp.where(mine, jnp.where(sub < 4, v, turned), 0.0))
            pieces.append(jnp.where(mine, jnp.where(sub < 4, turned, v), 0.0))
        blocks.append(jnp.concatenate(pieces, axis=1))
    flat = jnp.concatenate(blocks, axis=0) * 0.25
    at, lane = iota((512, 256), 0), iota((512, 256), 1)
    spread = (lane == 4 * (at & 63) + (at >> 7)).astype(BF16)
    top = flat.astype(BF16)
    rest = flat - top.astype(F32)
    mid = rest.astype(BF16)
    last = (rest - mid.astype(F32)).astype(BF16)
    out[...] = nn(top, spread) + (nn(mid, spread) + nn(last, spread))


def on_device(
    embedding,
    prompt_tile,
    crop_row,
    crop_col,
    points,
    confidence,
    pe_matrix,
    point_embed,
    w_one,
    w_two,
    w_three,
    conv_one,
    conv_two,
):
    early = is_early().astype(I32).reshape(1)
    smem = pl.BlockSpec(memory_space=pltpu.SMEM)
    vmem = pl.BlockSpec(memory_space=pltpu.VMEM)
    hbm = pl.BlockSpec(memory_space=pl.ANY)
    weights = (
        embedding.reshape(CELLS, C),
        conv_one,
        conv_two,
        pe_matrix,
        point_embed.reshape(1, 256),
        w_one,
        w_two,
        w_three,
    )
    up_shape = jax.ShapeDtypeStruct((16 * C2, CELLS), BF16)
    head_shape = jax.ShapeDtypeStruct((256, C2), BF16)
    scratch = [pltpu.VMEM(w.shape, w.dtype) for w in weights] + [
        pltpu.VMEM(up_shape.shape, BF16),
        pltpu.VMEM(head_shape.shape, BF16),
        pltpu.SemaphoreType.DMA((8,)),
    ]
    send, up, head = pl.pallas_call(
        slots_kernel,
        out_shape=(jax.ShapeDtypeStruct((NZ * NC, 1, 128), F32), up_shape, head_shape),
        in_specs=[smem] + [vmem] * 5 + [hbm] * 8,
        out_specs=(vmem, hbm, hbm),
        scratch_shapes=scratch,
    )(
        early,
        prompt_tile.reshape(1, P_DEV),
        crop_row.reshape(1, P_DEV),
        crop_col.reshape(1, P_DEV),
        points.T,
        confidence.reshape(1, P_DEV),
        *weights,
    )
    got = lax.all_to_all(send, ("z", "core"), 0, 0, tiled=True)
    up, head = pl.pallas_call(
        late_kernel,
        out_shape=(up_shape, head_shape),
        in_specs=[smem] + [hbm] * 10,
        out_specs=(hbm, hbm),
        scratch_shapes=scratch,
        input_output_aliases={1: 0, 2: 1},
    )(early, up, head, *weights)
    send = pl.pallas_call(
        regroup_kernel,
        out_shape=jax.ShapeDtypeStruct((NX * NR, 8, 128), BF16),
        in_specs=[vmem],
        out_specs=vmem,
    )(got)
    got = lax.all_to_all(send, ("x", "rep"), 0, 0, tiled=True)
    return pl.pallas_call(
        mask_kernel,
        out_shape=jax.ShapeDtypeStruct((4 * ROWS_T, 4 * EW), F32),
        in_specs=[vmem] * 3,
        out_specs=vmem,
    )(got, up, head)


def solution(mesh):
    split = Mesh(mesh.devices.reshape(NX, NZ, NC, NR), ("x", "z", "core", "rep"))
    tile, every = ("x", "z", "core"), ("x", "z", "core", "rep")
    return jax.shard_map(
        on_device,
        mesh=split,
        in_specs=(
            P(tile, None, None),
            P(every, None),
            P(every),
            P(every),
            P(every, None),
            P(every),
            P(),
            P(),
            P(),
            P(),
            P(),
            P(),
            P(),
        ),
        out_specs=P(tile, None),
        check_vma=False,
    )
```

time: 258 us -> 55.1 us (0.21)
  matrix products: 64.2 us -> 0 us
  waiting for transfers between devices: 64.4 us -> 6.39 us
  local copies, waits for them, and re-layouts: 53.2 us -> 2.05 us
  starting transfers between devices: 36.9 us -> 6.76 us
  blocking collectives: 0 us -> 25.7 us
  other arithmetic: 22.7 us -> 0 us
  Pallas kernels: 0 us -> 13.7 us
  between operations: 13.6 us -> 0.03 us
    dot_general x22 -> x0, matrix products: 64.2 us -> none  [the longest x4 43.4 us: mask_terms(): second = jnp.dot(active, conv_two, preferred_element_type=jnp.float32)]
    psum x1 -> x0, waiting for transfers between devices: 55.5 us -> none  [on_device(): summed = lax.psum(canvas, 'rep')]
    all_to_all x0 -> x1, blocking collectives: none -> 25.7 us  [on_device(): got = lax.all_to_all(send, ('z', 'core'), 0, 0, tiled=True)]
    all_to_all x2 -> x1, starting transfers between devices: 28.4 us -> 6.76 us  [on_device(): got = lax.all_to_all(send, ('x', 'rep'), 0, 0, tiled=True)]
    gather x2 -> x0, local copies, waits for them, and re-layouts: 16.7 us -> none  [cut_crops(): jnp.take(extended.reshape(height * width, channels), cell_index, axis=0)]
    reshape x12 -> x0, local copies, waits for them, and re-layouts: 14.9 us -> none  [the longest x4 13.1 us: mask_terms(): upscaled = jax.nn.gelu(second, approximate=False).astype(jnp.bfloat16).re...]
    pallas_call x0 -> x4, Pallas kernels: none -> 13.7 us  [the longest x1 8.87 us: on_device(): pl.pallas_call(slots_kernel, out_shape=(jax.ShapeDtypeStruct((NZ * NC, 1,...]
    reduce_sum x9 -> x0, other arithmetic: 8.38 us -> none  [the longest x4 5.13 us: mask_terms(): jnp.mean(centre * centre, axis=1, keepdims=True) + 1e-06]
  transfers between devices with their start and end apart: 5 -> 1, of which waited for: 3 -> 1; matrix products, arithmetic and copies ran while one was open for 11% -> 0% of each run, Pallas kernels for 0% -> 0%
where the time goes in v1:
time: 55.1 us; the launch traced here: 54.7 us
  blocking collectives  25.7 us (47%)
  Pallas kernels  13.7 us (25%)
  starting transfers between devices  6.76 us (12%)
  waiting for transfers between devices  6.39 us (12%)
  local copies, waits for them, and re-layouts  2.05 us (4%)
    all_to_all x1, blocking collectives, on_device(): got = lax.all_to_all(send, ('z', 'core'), 0, 0, tiled=True)  25.7 us
    pallas_call x1, Pallas kernels, on_device(): pl.pallas_call(slots_kernel, out_shape=(jax.ShapeDtypeStruct((NZ * NC, 1,...  8.87 us
    all_to_all x1, starting transfers between devices, on_device(): got = lax.all_to_all(send, ('x', 'rep'), 0, 0, tiled=True)  6.76 us
    all_to_all x1, waiting for transfers between devices, on_device(): got = lax.all_to_all(send, ('x', 'rep'), 0, 0, tiled=True)  6.39 us
    pallas_call x1, Pallas kernels, on_device(): pl.pallas_call(mask_kernel, out_shape=jax.ShapeDtypeStruct((4 * ROWS_T, 4...  3.3 us
    unnamed x3, local copies, waits for them, and re-layouts  2.05 us
    pallas_call x1, Pallas kernels, on_device(): pl.pallas_call(regroup_kernel, out_shape=jax.ShapeDtypeStruct((NX * NR, 8...  1.48 us
  transfers between devices with their start and end apart: 1, of which 1 were waited for; matrix products, arithmetic and copies ran while one was open for 0% of the time, Pallas kernels for 0%

profile of v1, /device:TPU:1, one launch (start us, length us, event | category | flops | bytes accessed | tf_op | source)
XLA Modules:
  0.0 54.7 jit_solution(16458783189023131321)
XLA Ops:
  0.0 1.4 %copy.16.rest_7_ = bf16[256,32]{1,0:T(8,128)(2,1)} copy(bf16[256,32]{0,1:T(8,128)(2,1)} %param.23) | data formatting | bytes 32768 | tf_op args[10]
  1.5 8.9 %shard_map.127 = (f32[32,1,128]{2,1,0:T(1,128)}, bf16[512,1024]{1,0:T(8,128)(2,1)}, bf16[256,32]{1,0:T(8,128)(2,1)}) custom-call(s32[1]{0:T(128)} %bitcast.early, s32[1,128]{1,0:T(1,128)} %bitcast.13, s32[1,128]{1,0:T(1,128)} %bitcast.14, s32[1,128]{1,0:T(1,128)} %bitcast.15, s32[2,128]{1,0:T(2,128)} %bitcast.12, s32[1,128]{1,0:T(1,128)} %bitcast.16, ...), custom_call_target="tpu_custom_call" | custom-call | tf_op jit(solution)/shard_map/pallas_call | solution.py:257
  10.3 25.7 %all_to_all.10.got = f32[32,1,128]{2,1,0:T(1,128)} all-to-all(f32[32,1,128]{2,1,0:T(1,128)} %get-tuple-element.10), channel_id=1, replica_groups=mesh['x'=4,'z'=16,'core'=2,'rep'=4] {'z','core'}, dimensions={0} | all-to-all | bytes 32768 | tf_op jit(solution)/shard_map/all_to_all | solution.py:272
  36.0 1.5 %shard_map.128 = bf16[16,8,128]{2,1,0:T(8,128)(2,1)} custom-call(f32[32,1,128]{2,1,0:T(1,128)} %all_to_all.10.got), custom_call_target="tpu_custom_call" | custom-call | tf_op jit(solution)/shard_map/pallas_call | solution.py:281
  37.5 6.8 %all-to-all-start.1 = ((bf16[16,8,128]{2,1,0:T(8,128)(2,1)}), bf16[16,8,128]{2,1,0:T(8,128)(2,1)S(1)}, u32[]{:S(2)}, u32[]{:S(2)}) async-start(bf16[16,8,128]{2,1,0:T(8,128)(2,1)} %shard_map.128), calls=%async_computation.1 | async-start | bytes 65536 | tf_op jit(solution)/shard_map/all_to_all | solution.py:287
  44.3 0.1 shard_map.129
  44.4 6.4 %all-to-all-done.1.got = bf16[16,8,128]{2,1,0:T(8,128)(2,1)S(1)} async-done(((bf16[16,8,128]{2,1,0:T(8,128)(2,1)}), bf16[16,8,128]{2,1,0:T(8,128)(2,1)S(1)}, u32[]{:S(2)}, u32[]{:S(2)}) %all-to-all-start.1) | async-done | bytes 32800 | tf_op jit(solution)/shard_map/all_to_all | solution.py:287
  50.7 0.0 copy-start
  50.7 0.6 %copy-done = bf16[16,8,128]{2,1,0:T(8,128)(2,1)} copy-done((bf16[16,8,128]{2,1,0:T(8,128)(2,1)}, bf16[16,8,128]{2,1,0:T(8,128)(2,1)S(1)}, u32[]{:S(2)}) %copy-start) | copy-done | bytes 32792
  51.4 3.3 %shard_map.130 = f32[64,256]{1,0:T(8,128)} custom-call(bf16[16,8,128]{2,1,0:T(8,128)(2,1)} %copy-done, bf16[512,1024]{1,0:T(8,128)(2,1)} %get-tuple-element.13.up, bf16[256,32]{1,0:T(8,128)(2,1)} %get-tuple-element.14.head), custom_call_target="tpu_custom_call" | custom-call | tf_op jit(solution)/shard_map/pallas_call | solution.py:288
Async XLA Ops:
  37.5 13.3 %all-to-all-start.1 = ((bf16[16,8,128]{2,1,0:T(8,128)(2,1)}), bf16[16,8,128]{2,1,0:T(8,128)(2,1)S(1)}, u32[]{:S(2)}, u32[]{:S(2)}) async-start(bf16[16,8,128]{2,1,0:T(8,128)(2,1)} %shard_map.128), calls=%async_computation.1 | async-start | bytes 65536 | tf_op jit(solution)/shard_map/all_to_all | solution.py:287
  50.7 0.6 %copy-start = (bf16[16,8,128]{2,1,0:T(8,128)(2,1)}, bf16[16,8,128]{2,1,0:T(8,128)(2,1)S(1)}, u32[]{:S(2)}) copy-start(bf16[16,8,128]{2,1,0:T(8,128)(2,1)S(1)} %all-to-all-done.1.got) | copy-start | bytes 98308

commit v2 on v1

--- a/solution.py
+++ b/solution.py
@@ -47,7 +47,7 @@
     tokens = (jnp.concatenate([jnp.sin(angles), jnp.cos(angles)], axis=1) + bias[...]).astype(BF16)
     hidden = jnp.maximum(nn(tokens, w1[...]), 0.0).astype(BF16)
     hidden = jnp.maximum(nn(hidden, w2[...]), 0.0).astype(BF16)
-    head_ref[...] = nn(hidden, w3[...]).astype(BF16)
+    head_ref[...] = nt(w3[...], hidden).astype(BF16)
 
     row = iota((512, P_DEV), 0)
     k, x, y = row >> 4, (row >> 2) & 3, row & 3
@@ -83,25 +83,17 @@
         c.wait()
 
 
-def store_out(up_buf, head_buf, up_ref, head_ref, sems):
-    copies = [
-        pltpu.make_async_copy(up_buf, up_ref, sems.at[0]),
-        pltpu.make_async_copy(head_buf, head_ref, sems.at[1]),
-    ]
-    for c in copies:
-        c.start()
-    for c in copies:
-        c.wait()
+def in_vmem(value):
+    return pltpu.with_memory_space_constraint(value, pltpu.VMEM)
 
 
 def is_early():
-    z = lax.axis_index("z")
-    return (z <= 4) | (z >= 12)
+    return lax.axis_index("z") <= 3
 
 
 def slots_kernel(early, tile, row, col, pts, conf, *rest):
     weights, (send, up, head), scratch = rest[:8], rest[8:11], rest[11:]
-    bufs, (up_buf, head_buf, sems) = scratch[:8], scratch[8:]
+    bufs, sems = scratch[:8], scratch[8]
     t = tile[...]
     names = (iota((P_DEV, P_DEV), 0) == t).astype(F32)
     before = (iota((P_DEV, P_DEV), 0) < iota((P_DEV, P_DEV), 1)).astype(BF16)
@@ -126,19 +118,17 @@
     @pl.when(early[0] == 1)
     def _():
         gathered_in(weights, bufs, sems)
-        local_tables(*bufs, up_buf, head_buf)
-        store_out(up_buf, head_buf, up, head, sems)
+        local_tables(*bufs, up, head)
 
 
 def late_kernel(early, up_in, head_in, *rest):
     weights, (up, head), scratch = rest[:8], rest[8:10], rest[10:]
-    bufs, (up_buf, head_buf, sems) = scratch[:8], scratch[8:]
+    bufs, sems = scratch[:8], scratch[8]
 
     @pl.when(early[0] != 1)
     def _():
         gathered_in(weights, bufs, sems)
-        local_tables(*bufs, up_buf, head_buf)
-        store_out(up_buf, head_buf, up, head, sems)
+        local_tables(*bufs, up, head)
 
 
 def regroup_kernel(got, send):
@@ -174,8 +164,7 @@
         row, col, conf, first, second = (v[i : i + 1, :] for i in range(5))
         hot_a, hot_b = one_hot(first, r_at), one_hot(second, r_at)
         hot = jnp.concatenate([hot_a[i : i + 1, :] * hot_b for i in range(16)], axis=0)
-        heads = lax.dot_general(table, hot, (((0,), (0,)), ((), ())), preferred_element_type=F32)
-        heads = heads.astype(BF16)
+        heads = nn(table, hot).astype(BF16)
         d = r_at - row
         in_row = ((d >= 0.0) & (d <= 3.0)).astype(BF16)
         d = c_at - col
@@ -245,20 +234,16 @@
         point_embed.reshape(1, 256),
         w_one,
         w_two,
-        w_three,
+        w_three.T,
     )
-    up_shape = jax.ShapeDtypeStruct((16 * C2, CELLS), BF16)
-    head_shape = jax.ShapeDtypeStruct((256, C2), BF16)
-    scratch = [pltpu.VMEM(w.shape, w.dtype) for w in weights] + [
-        pltpu.VMEM(up_shape.shape, BF16),
-        pltpu.VMEM(head_shape.shape, BF16),
-        pltpu.SemaphoreType.DMA((8,)),
-    ]
+    up_shape = pltpu.VMEM((16 * C2, CELLS), BF16)
+    head_shape = pltpu.VMEM((C2, 256), BF16)
+    scratch = [pltpu.VMEM(w.shape, w.dtype) for w in weights] + [pltpu.SemaphoreType.DMA((8,))]
     send, up, head = pl.pallas_call(
         slots_kernel,
-        out_shape=(jax.ShapeDtypeStruct((NZ * NC, 1, 128), F32), up_shape, head_shape),
+        out_shape=(pltpu.VMEM((NZ * NC, 1, 128), F32), up_shape, head_shape),
         in_specs=[smem] + [vmem] * 5 + [hbm] * 8,
-        out_specs=(vmem, hbm, hbm),
+        out_specs=(vmem, vmem, vmem),
         scratch_shapes=scratch,
     )(
         early,
@@ -273,24 +258,24 @@
     up, head = pl.pallas_call(
         late_kernel,
         out_shape=(up_shape, head_shape),
-        in_specs=[smem] + [hbm] * 10,
-        out_specs=(hbm, hbm),
+        in_specs=[smem] + [vmem] * 2 + [hbm] * 8,
+        out_specs=(vmem, vmem),
         scratch_shapes=scratch,
         input_output_aliases={1: 0, 2: 1},
-    )(early, up, head, *weights)
-    send = pl.pallas_call(
+    )(early, in_vmem(up), in_vmem(head), *weights)
+    (send,) = pl.pallas_call(
         regroup_kernel,
-        out_shape=jax.ShapeDtypeStruct((NX * NR, 8, 128), BF16),
+        out_shape=(pltpu.VMEM((NX * NR, 8, 128), BF16),),
         in_specs=[vmem],
-        out_specs=vmem,
-    )(got)
+        out_specs=(vmem,),
+    )(in_vmem(got))
     got = lax.all_to_all(send, ("x", "rep"), 0, 0, tiled=True)
     return pl.pallas_call(
         mask_kernel,
         out_shape=jax.ShapeDtypeStruct((4 * ROWS_T, 4 * EW), F32),
         in_specs=[vmem] * 3,
         out_specs=vmem,
-    )(got, up, head)
+    )(in_vmem(got), in_vmem(up), in_vmem(head))
 
 
 def solution(mesh):

time: 55.1 us -> 45.8 us (0.83)
  Pallas kernels: 13.7 us -> 10.2 us
  blocking collectives: 25.7 us -> 22.2 us
  local copies, waits for them, and re-layouts: 2.05 us -> 0 us
    all_to_all x1, blocking collectives: 25.7 us -> 22.2 us  [on_device(): got = lax.all_to_all(send, ('z', 'core'), 0, 0, tiled=True)]
    pallas_call x2, Pallas kernels: 10.3 us -> 8.02 us  [the longest x1 7.24 us: on_device(): pl.pallas_call(slots_kernel, out_shape=(pltpu.VMEM((NZ * NC, 1, 128), F32...]
    unnamed x3 -> x0, local copies, waits for them, and re-layouts: 2.05 us -> none
    pallas_call x1, Pallas kernels: 3.3 us -> 2.05 us  [on_device(): pl.pallas_call(mask_kernel, out_shape=jax.ShapeDtypeStruct((4 * ROWS_T, 4...]
where the time goes in v2:
time: 45.8 us; the launch traced here: 45.5 us
  blocking collectives  22.2 us (48%)
  Pallas kernels  10.2 us (22%)
  starting transfers between devices  6.75 us (15%)
  waiting for transfers between devices  6.38 us (14%)
    all_to_all x1, blocking collectives, on_device(): got = lax.all_to_all(send, ('z', 'core'), 0, 0, tiled=True)  22.2 us
    pallas_call x1, Pallas kernels, on_device(): pl.pallas_call(slots_kernel, out_shape=(pltpu.VMEM((NZ * NC, 1, 128), F32...  7.24 us
    all_to_all x1, starting transfers between devices, on_device(): got = lax.all_to_all(send, ('x', 'rep'), 0, 0, tiled=True)  6.75 us
    all_to_all x1, waiting for transfers between devices, on_device(): got = lax.all_to_all(send, ('x', 'rep'), 0, 0, tiled=True)  6.38 us
    pallas_call x1, Pallas kernels, on_device(): pl.pallas_call(mask_kernel, out_shape=jax.ShapeDtypeStruct((4 * ROWS_T, 4...  2.05 us
  transfers between devices with their start and end apart: 1, of which 1 were waited for; matrix products, arithmetic and copies ran while one was open for 0% of the time, Pallas kernels for 0%

profile of v2, /device:TPU:1, one launch (start us, length us, event | category | flops | bytes accessed | tf_op | source)
XLA Modules:
  0.0 45.5 jit_solution(17709667757274201726)
XLA Ops:
  0.0 7.2 %shard_map.127 = (f32[32,1,128]{2,1,0:T(1,128)S(1)}, bf16[512,1024]{1,0:T(8,128)(2,1)S(1)}, bf16[32,256]{1,0:T(8,128)(2,1)S(1)}) custom-call(s32[1]{0:T(128)} %bitcast.early, s32[1,128]{1,0:T(1,128)} %bitcast.16, s32[1,128]{1,0:T(1,128)} %bitcast.17, s32[1,128]{1,0:T(1,128)} %bitcast.18, s32[2,128]{1,0:T(2,128)} %bitcast.15, s32[1,128]{1,0:T(1,128)} %bitcast.19, ...), custom_call_target="tpu_custom_call" | custom-call | tf_op jit(solution)/shard_map/pallas_call | solution.py:242
  7.3 22.2 %all_to_all.10.got = f32[32,1,128]{2,1,0:T(1,128)S(1)} all-to-all(f32[32,1,128]{2,1,0:T(1,128)S(1)} %get-tuple-element.10), channel_id=1, replica_groups=mesh['x'=4,'z'=16,'core'=2,'rep'=4] {'z','core'}, dimensions={0} | all-to-all | bytes 32768 | tf_op jit(solution)/shard_map/all_to_all | solution.py:257
  29.5 0.8 %shard_map.128 = bf16[16,8,128]{2,1,0:T(8,128)(2,1)} custom-call(f32[32,1,128]{2,1,0:T(1,128)S(1)} %all_to_all.10.got), custom_call_target="tpu_custom_call" | custom-call | tf_op jit(solution)/shard_map/pallas_call | solution.py:266
  30.2 6.8 %all-to-all-start.1 = ((bf16[16,8,128]{2,1,0:T(8,128)(2,1)}), bf16[16,8,128]{2,1,0:T(8,128)(2,1)S(1)}, u32[]{:S(2)}, u32[]{:S(2)}) async-start(bf16[16,8,128]{2,1,0:T(8,128)(2,1)} %shard_map.128), calls=%async_computation.1 | async-start | bytes 65536 | tf_op jit(solution)/shard_map/all_to_all | solution.py:272
  37.0 0.1 shard_map.129
  37.1 6.4 %all-to-all-done.1.got = bf16[16,8,128]{2,1,0:T(8,128)(2,1)S(1)} async-done(((bf16[16,8,128]{2,1,0:T(8,128)(2,1)}), bf16[16,8,128]{2,1,0:T(8,128)(2,1)S(1)}, u32[]{:S(2)}, u32[]{:S(2)}) %all-to-all-start.1) | async-done | bytes 32800 | tf_op jit(solution)/shard_map/all_to_all | solution.py:272
  43.5 2.1 %shard_map.130 = f32[64,256]{1,0:T(8,128)} custom-call(bf16[16,8,128]{2,1,0:T(8,128)(2,1)S(1)} %all-to-all-done.1.got, bf16[512,1024]{1,0:T(8,128)(2,1)S(1)} %get-tuple-element.13.up, bf16[32,256]{1,0:T(8,128)(2,1)S(1)} %get-tuple-element.14.head), custom_call_target="tpu_custom_call" | custom-call | tf_op jit(solution)/shard_map/pallas_call | solution.py:273
Async XLA Ops:
  30.2 13.2 %all-to-all-start.1 = ((bf16[16,8,128]{2,1,0:T(8,128)(2,1)}), bf16[16,8,128]{2,1,0:T(8,128)(2,1)S(1)}, u32[]{:S(2)}, u32[]{:S(2)}) async-start(bf16[16,8,128]{2,1,0:T(8,128)(2,1)} %shard_map.128), calls=%async_computation.1 | async-start | bytes 65536 | tf_op jit(solution)/shard_map/all_to_all | solution.py:272

commit v3 on v2

--- a/solution.py
+++ b/solution.py
@@ -17,6 +17,8 @@
 P_DEV = 128
 NX, NZ, NC, NR = 4, 16, 2, 4
 CELLS = ROWS_T * EW
+Z_FIRST, C_FIRST, X_FIRST, R_FIRST = 8, 1, 2, 2
+EVERY = ("x", "z", "core", "rep")
 F32 = jnp.float32
 BF16 = jnp.bfloat16
 I32 = jnp.int32
@@ -24,6 +26,30 @@
 
 def iota(shape, dim):
     return lax.broadcasted_iota(I32, shape, dim)
+
+
+def flat(x, z, c, r):
+    return ((x % NX * NZ + z % NZ) * NC + c % NC) * NR + r % NR
+
+
+def exchanged(value, groups):
+    return lax.all_to_all(value, EVERY, 0, 0, axis_index_groups=groups, tiled=True)
+
+
+def column_groups():
+    return [
+        [flat(x, Z_FIRST + i, C_FIRST + j, r) for i in range(NZ) for j in range(NC)]
+        for x in range(NX)
+        for r in range(NR)
+    ]
+
+
+def plane_groups():
+    return [
+        [flat(X_FIRST + i, z, c, R_FIRST + j) for i in range(NX) for j in range(NR)]
+        for z in range(NZ)
+        for c in range(NC)
+    ]
 
 
 def nt(a, b):
@@ -88,7 +114,7 @@
 
 
 def is_early():
-    return lax.axis_index("z") <= 3
+    return lax.axis_index("z") <= 2
 
 
 def slots_kernel(early, tile, row, col, pts, conf, *rest):
@@ -108,9 +134,9 @@
         mask = ((target >> 5) == x_of) & (rank_at == s_of)
         rows = [jnp.where(mask, v.astype(F32), 0.0) for v in values]
         rows += [jnp.zeros((16, P_DEV), F32)] * 3
-        return nt(
-            ((target & 31) == dest).astype(BF16), jnp.concatenate(rows, axis=0).astype(BF16)
-        )
+        z, c = (target >> 1) - Z_FIRST, target - C_FIRST
+        place = 2 * (z & 15) + (c & 1)
+        return nt((place == dest).astype(BF16), jnp.concatenate(rows, axis=0).astype(BF16))
 
     out = part(t, rank, values) + part(t + 1, rank + 2, [values[0] - ROWS_T] + values[1:])
     send[...] = out.reshape(NZ * NC, 1, 128)
@@ -139,9 +165,10 @@
     at, lane = iota((32, 128), 0), iota((32, 128), 1)
     pick = ((lane >> 4) == (at & 7)) & (((lane >> 2) & 3) == (at >> 3))
     out = nt(pick.astype(BF16), r)
-    for x in range(NX):
-        for y in range(NR):
-            send[x * NR + y] = out[x * 8 : (x + 1) * 8, :].astype(BF16)
+    for i in range(NX):
+        x = (X_FIRST + i) % NX
+        for j in range(NR):
+            send[i * NR + j] = out[x * 8 : (x + 1) * 8, :].astype(BF16)
 
 
 def mask_kernel(got, up, head, out):
@@ -254,7 +281,7 @@
         confidence.reshape(1, P_DEV),
         *weights,
     )
-    got = lax.all_to_all(send, ("z", "core"), 0, 0, tiled=True)
+    got = exchanged(send, column_groups())
     up, head = pl.pallas_call(
         late_kernel,
         out_shape=(up_shape, head_shape),
@@ -269,7 +296,7 @@
         in_specs=[vmem],
         out_specs=(vmem,),
     )(in_vmem(got))
-    got = lax.all_to_all(send, ("x", "rep"), 0, 0, tiled=True)
+    got = exchanged(send, plane_groups())
     return pl.pallas_call(
         mask_kernel,
         out_shape=jax.ShapeDtypeStruct((4 * ROWS_T, 4 * EW), F32),
@@ -279,8 +306,8 @@
 
 
 def solution(mesh):
-    split = Mesh(mesh.devices.reshape(NX, NZ, NC, NR), ("x", "z", "core", "rep"))
-    tile, every = ("x", "z", "core"), ("x", "z", "core", "rep")
+    split = Mesh(mesh.devices.reshape(NX, NZ, NC, NR), EVERY)
+    tile, every = EVERY[:3], EVERY
     return jax.shard_map(
         on_device,
         mesh=split,

time: 45.8 us -> 42 us (0.917)
  the two profiles are of different devices: /device:TPU:1 before, /device:TPU:96 now
where the time goes in v3:
time: 42 us; the launch traced here: 41.8 us
  blocking collectives  24.4 us (58%)
  Pallas kernels  10.1 us (24%)
  starting transfers between devices  7.23 us (17%)
    all_to_all x1, blocking collectives, exchanged(): lax.all_to_all(value, EVERY, 0, 0, axis_index_groups=groups, tiled=True)  24.4 us
    all_to_all x1, starting transfers between devices, exchanged(): lax.all_to_all(value, EVERY, 0, 0, axis_index_groups=groups, tiled=True)  7.23 us
    pallas_call x1, Pallas kernels, on_device(): pl.pallas_call(late_kernel, out_shape=(up_shape, head_shape), in_specs=[s...  6.21 us
    pallas_call x1, Pallas kernels, on_device(): pl.pallas_call(mask_kernel, out_shape=jax.ShapeDtypeStruct((4 * ROWS_T, 4...  2.06 us
    pallas_call x1, Pallas kernels, on_device(): pl.pallas_call(slots_kernel, out_shape=(pltpu.VMEM((NZ * NC, 1, 128), F32...  1.1 us
  transfers between devices with their start and end apart: 1, of which 0 were waited for; matrix products, arithmetic and copies ran while one was open for 0% of the time, Pallas kernels for 15%

profile of v3, /device:TPU:96, one launch (start us, length us, event | category | flops | bytes accessed | tf_op | source)
XLA Modules:
  0.0 41.8 jit_solution(1727274710139740304)
XLA Ops:
  0.0 1.1 %shard_map.127 = (f32[32,1,128]{2,1,0:T(1,128)S(1)}, bf16[512,1024]{1,0:T(8,128)(2,1)S(1)}, bf16[32,256]{1,0:T(8,128)(2,1)S(1)}) custom-call(s32[1]{0:T(128)} %bitcast.early, s32[1,128]{1,0:T(1,128)} %bitcast.16, s32[1,128]{1,0:T(1,128)} %bitcast.17, s32[1,128]{1,0:T(1,128)} %bitcast.18, s32[2,128]{1,0:T(2,128)} %bitcast.15, s32[1,128]{1,0:T(1,128)} %bitcast.19, ...), custom_call_target="tpu_custom_call" | custom-call | tf_op jit(solution)/shard_map/pallas_call | solution.py:269
  1.1 24.4 %all_to_all.10.got = f32[32,1,128]{2,1,0:T(1,128)S(1)} all-to-all(f32[32,1,128]{2,1,0:T(1,128)S(1)} %get-tuple-element.10), channel_id=1, replica_groups={{68,64,76,72,84,80,92,88,100,96,108,104,116,112,124,120,4,0,12,8,20,16,..., dimensions={0} | all-to-all | bytes 32768 | tf_op jit(solution)/shard_map/all_to_all | solution.py:36
  25.5 0.8 %shard_map.128 = bf16[16,8,128]{2,1,0:T(8,128)(2,1)} custom-call(f32[32,1,128]{2,1,0:T(1,128)S(1)} %all_to_all.10.got), custom_call_target="tpu_custom_call" | custom-call | tf_op jit(solution)/shard_map/pallas_call | solution.py:293
  26.2 7.2 %all-to-all-start.1 = ((bf16[16,8,128]{2,1,0:T(8,128)(2,1)}), bf16[16,8,128]{2,1,0:T(8,128)(2,1)S(1)}, u32[]{:S(2)}, u32[]{:S(2)}) async-start(bf16[16,8,128]{2,1,0:T(8,128)(2,1)} %shard_map.128), calls=%async_computation.1 | async-start | bytes 65536 | tf_op jit(solution)/shard_map/all_to_all | solution.py:36
  33.5 6.2 %shard_map.129 = (bf16[512,1024]{1,0:T(8,128)(2,1)S(1)}, bf16[32,256]{1,0:T(8,128)(2,1)S(1)}) custom-call(s32[1]{0:T(128)} %bitcast.early, bf16[512,1024]{1,0:T(8,128)(2,1)S(1)} %get-tuple-element.11.up_in, bf16[32,256]{1,0:T(8,128)(2,1)S(1)} %get-tuple-element.12.head_in, bf16[1024,256]{1,0:T(8,128)(2,1)} %bitcast.10, ...), custom_call_target="tpu_custom_call", output_to_operand_aliasing={{0}: (1, {}), {1}: (2, {})} | custom-call | tf_op jit(solution)/shard_map/pallas_call | solution.py:285
  39.7 0.0 all-to-all-done.1.got
  39.7 2.1 %shard_map.130 = f32[64,256]{1,0:T(8,128)} custom-call(bf16[16,8,128]{2,1,0:T(8,128)(2,1)S(1)} %all-to-all-done.1.got, bf16[512,1024]{1,0:T(8,128)(2,1)S(1)} %get-tuple-element.13.up, bf16[32,256]{1,0:T(8,128)(2,1)S(1)} %get-tuple-element.14.head), custom_call_target="tpu_custom_call" | custom-call | tf_op jit(solution)/shard_map/pallas_call | solution.py:300
Async XLA Ops:
  26.2 13.5 %all-to-all-start.1 = ((bf16[16,8,128]{2,1,0:T(8,128)(2,1)}), bf16[16,8,128]{2,1,0:T(8,128)(2,1)S(1)}, u32[]{:S(2)}, u32[]{:S(2)}) async-start(bf16[16,8,128]{2,1,0:T(8,128)(2,1)} %shard_map.128), calls=%async_computation.1 | async-start | bytes 65536 | tf_op jit(solution)/shard_map/all_to_all | solution.py:36

commit v4 on v3

--- a/solution.py
+++ b/solution.py
@@ -114,7 +114,8 @@
 
 
 def is_early():
-    return lax.axis_index("z") <= 2
+    at = [lax.axis_index(a) for a in EVERY]
+    return (at[1] <= 3) & (at[0] + at[1] + at[2] + at[3] > 0)
 
 
 def slots_kernel(early, tile, row, col, pts, conf, *rest):

time: 42 us -> 39.3 us (0.936)
  the two profiles are of different devices: /device:TPU:96 before, /device:TPU:128 now
where the time goes in v4:
time: 39.3 us; the launch traced here: 39.1 us
  blocking collectives  19.9 us (51%)
  Pallas kernels  10.1 us (26%)
  starting transfers between devices  9 us (23%)
    all_to_all x1, blocking collectives, exchanged(): lax.all_to_all(value, EVERY, 0, 0, axis_index_groups=groups, tiled=True)  19.9 us
    all_to_all x1, starting transfers between devices, exchanged(): lax.all_to_all(value, EVERY, 0, 0, axis_index_groups=groups, tiled=True)  9 us
    pallas_call x1, Pallas kernels, on_device(): pl.pallas_call(late_kernel, out_shape=(up_shape, head_shape), in_specs=[s...  6.21 us
    pallas_call x1, Pallas kernels, on_device(): pl.pallas_call(mask_kernel, out_shape=jax.ShapeDtypeStruct((4 * ROWS_T, 4...  2.05 us
    pallas_call x1, Pallas kernels, on_device(): pl.pallas_call(slots_kernel, out_shape=(pltpu.VMEM((NZ * NC, 1, 128), F32...  1.1 us
  transfers between devices with their start and end apart: 1, of which 0 were waited for; matrix products, arithmetic and copies ran while one was open for 0% of the time, Pallas kernels for 16%

profile of v4, /device:TPU:128, one launch (start us, length us, event | category | flops | bytes accessed | tf_op | source)
XLA Modules:
  0.0 39.1 jit_solution(17576246288106938949)
XLA Ops:
  0.0 1.1 %shard_map.127 = (f32[32,1,128]{2,1,0:T(1,128)S(1)}, bf16[512,1024]{1,0:T(8,128)(2,1)S(1)}, bf16[32,256]{1,0:T(8,128)(2,1)S(1)}) custom-call(s32[1]{0:T(128)} %bitcast.early, s32[1,128]{1,0:T(1,128)} %bitcast.16, s32[1,128]{1,0:T(1,128)} %bitcast.17, s32[1,128]{1,0:T(1,128)} %bitcast.18, s32[2,128]{1,0:T(2,128)} %bitcast.15, s32[1,128]{1,0:T(1,128)} %bitcast.19, ...), custom_call_target="tpu_custom_call" | custom-call | tf_op jit(solution)/shard_map/pallas_call | solution.py:270
  1.1 19.9 %all_to_all.10.got = f32[32,1,128]{2,1,0:T(1,128)S(1)} all-to-all(f32[32,1,128]{2,1,0:T(1,128)S(1)} %get-tuple-element.10), channel_id=1, replica_groups={{68,64,76,72,84,80,92,88,100,96,108,104,116,112,124,120,4,0,12,8,20,16,..., dimensions={0} | all-to-all | bytes 32768 | tf_op jit(solution)/shard_map/all_to_all | solution.py:36
  21.0 0.8 %shard_map.128 = bf16[16,8,128]{2,1,0:T(8,128)(2,1)} custom-call(f32[32,1,128]{2,1,0:T(1,128)S(1)} %all_to_all.10.got), custom_call_target="tpu_custom_call" | custom-call | tf_op jit(solution)/shard_map/pallas_call | solution.py:294
  21.8 9.0 %all-to-all-start.1 = ((bf16[16,8,128]{2,1,0:T(8,128)(2,1)}), bf16[16,8,128]{2,1,0:T(8,128)(2,1)S(1)}, u32[]{:S(2)}, u32[]{:S(2)}) async-start(bf16[16,8,128]{2,1,0:T(8,128)(2,1)} %shard_map.128), calls=%async_computation.1 | async-start | bytes 65536 | tf_op jit(solution)/shard_map/all_to_all | solution.py:36
  30.8 6.2 %shard_map.129 = (bf16[512,1024]{1,0:T(8,128)(2,1)S(1)}, bf16[32,256]{1,0:T(8,128)(2,1)S(1)}) custom-call(s32[1]{0:T(128)} %bitcast.early, bf16[512,1024]{1,0:T(8,128)(2,1)S(1)} %get-tuple-element.11.up_in, bf16[32,256]{1,0:T(8,128)(2,1)S(1)} %get-tuple-element.12.head_in, bf16[1024,256]{1,0:T(8,128)(2,1)} %bitcast.10, ...), custom_call_target="tpu_custom_call", output_to_operand_aliasing={{0}: (1, {}), {1}: (2, {})} | custom-call | tf_op jit(solution)/shard_map/pallas_call | solution.py:286
  37.0 0.0 all-to-all-done.1.got
  37.0 2.1 %shard_map.130 = f32[64,256]{1,0:T(8,128)} custom-call(bf16[16,8,128]{2,1,0:T(8,128)(2,1)S(1)} %all-to-all-done.1.got, bf16[512,1024]{1,0:T(8,128)(2,1)S(1)} %get-tuple-element.13.up, bf16[32,256]{1,0:T(8,128)(2,1)S(1)} %get-tuple-element.14.head), custom_call_target="tpu_custom_call" | custom-call | tf_op jit(solution)/shard_map/pallas_call | solution.py:301
Async XLA Ops:
  21.8 15.2 %all-to-all-start.1 = ((bf16[16,8,128]{2,1,0:T(8,128)(2,1)}), bf16[16,8,128]{2,1,0:T(8,128)(2,1)S(1)}, u32[]{:S(2)}, u32[]{:S(2)}) async-start(bf16[16,8,128]{2,1,0:T(8,128)(2,1)} %shard_map.128), calls=%async_computation.1 | async-start | bytes 65536 | tf_op jit(solution)/shard_map/all_to_all | solution.py:36

commit v5 on v4

--- a/solution.py
+++ b/solution.py
@@ -18,6 +18,7 @@
 NX, NZ, NC, NR = 4, 16, 2, 4
 CELLS = ROWS_T * EW
 Z_FIRST, C_FIRST, X_FIRST, R_FIRST = 8, 1, 2, 2
+UNROLL, BLOCK = 4, 256
 EVERY = ("x", "z", "core", "rep")
 F32 = jnp.float32
 BF16 = jnp.bfloat16
@@ -65,29 +66,35 @@
 
 
 def local_tables(emb, one, two, pe, bias, w1, w2, w3, up_ref, head_ref):
-    q = iota((256, P_DEV), 0)
-    first = ((q >> 4).astype(F32) + 0.5) / (4.0 * CK) * 2.0 - 1.0
-    second = ((q & 15).astype(F32) + 0.5) / (4.0 * CK) * 2.0 - 1.0
-    pe_value = pe[...]
-    angles = (first * pe_value[0:1, :] + second * pe_value[1:2, :]) * (2.0 * math.pi)
-    tokens = (jnp.concatenate([jnp.sin(angles), jnp.cos(angles)], axis=1) + bias[...]).astype(BF16)
+    coord = (iota((16, P_DEV), 0).astype(F32) + 0.5) / (4.0 * CK) * 2.0 - 1.0
+    angle_a = coord * pe[0:1, :] * (2.0 * math.pi)
+    angle_b = coord * pe[1:2, :] * (2.0 * math.pi)
+    sin_a, cos_a, sin_b, cos_b = jnp.sin(angle_a), jnp.cos(angle_a), jnp.sin(angle_b), jnp.cos(angle_b)
+    sines, cosines = [], []
+    for i in range(16):
+        sin_i, cos_i = sin_a[i : i + 1, :], cos_a[i : i + 1, :]
+        sines.append(sin_i * cos_b + cos_i * sin_b)
+        cosines.append(cos_i * cos_b - sin_i * sin_b)
+    sines, cosines = jnp.concatenate(sines, axis=0), jnp.concatenate(cosines, axis=0)
+    tokens = (jnp.concatenate([sines, cosines], axis=1) + bias[...]).astype(BF16)
     hidden = jnp.maximum(nn(tokens, w1[...]), 0.0).astype(BF16)
     hidden = jnp.maximum(nn(hidden, w2[...]), 0.0).astype(BF16)
     head_ref[...] = nt(w3[...], hidden).astype(BF16)
 
-    row = iota((512, P_DEV), 0)
-    k, x, y = row >> 4, (row >> 2) & 3, row & 3
-    pick = (iota((512, P_DEV), 1) == (2 * (y & 1) + (x & 1)) * C2 + k).astype(BF16)
-    row = iota((512, 256), 0)
-    off = 2 * ((row & 3) >> 1) + (((row >> 2) & 3) >> 1)
-    keep = (iota((512, 256), 1) >> 6) == off
-    two_tiled = jnp.concatenate([two[...]] * 4, axis=0)
-    wide = jnp.where(keep, nt(pick, two_tiled), 0.0).astype(BF16)
+    row = iota((16, P_DEV), 0)
+    x, y = row >> 2, row & 3
+    ahead = iota((16, P_DEV), 1) - (2 * (y & 1) + (x & 1)) * C2
+    pick = jnp.concatenate([(ahead == k).astype(F32) for k in range(C2)], axis=0).astype(BF16)
+    row = iota((16, 256), 0)
+    keep = (iota((16, 256), 1) >> 6) == 2 * ((row & 3) >> 1) + (row >> 3)
+    spread = nt(pick, jnp.concatenate([two[...]] * 4, axis=0))
+    wide = [jnp.where(keep, spread[16 * k : 16 * k + 16], 0.0) for k in range(C2)]
+    wide = jnp.concatenate(wide, axis=0).astype(BF16)
     one_t = one[...].astype(F32).T.astype(BF16)
 
     def block(i, carry):
-        start = pl.multiple_of(i * 128, 128)
-        first_up = nt(one_t, emb[pl.ds(start, 128), :])
+        start = pl.multiple_of(i * BLOCK, BLOCK)
+        first_up = nt(one_t, emb[pl.ds(start, BLOCK), :])
         parts = []
         for o in range(4):
             v = first_up[o * C1 : (o + 1) * C1, :]
@@ -95,10 +102,10 @@
             v = v * lax.rsqrt(jnp.mean(v * v, axis=0, keepdims=True) + 1e-06)
             parts.append(gelu(v).astype(BF16))
         active = jnp.concatenate(parts, axis=0)
-        up_ref[:, pl.ds(start, 128)] = gelu(nn(wide, active)).astype(BF16)
+        up_ref[:, pl.ds(start, BLOCK)] = gelu(nn(wide, active)).astype(BF16)
         return carry
 
-    lax.fori_loop(0, CELLS // 128, block, 0)
+    lax.fori_loop(0, CELLS // BLOCK, block, 0, unroll=UNROLL)
 
 
 def gathered_in(refs, bufs, sems):
@@ -115,7 +122,7 @@
 
 def is_early():
     at = [lax.axis_index(a) for a in EVERY]
-    return (at[1] <= 3) & (at[0] + at[1] + at[2] + at[3] > 0)
+    return (at[1] <= 7) & (at[0] + at[1] + at[2] + at[3] > 0)
 
 
 def slots_kernel(early, tile, row, col, pts, conf, *rest):
@@ -158,7 +165,8 @@
         local_tables(*bufs, up, head)
 
 
-def regroup_kernel(got, send):
+def regroup_kernel(got, send, spare):
+    spare[...] = jnp.zeros((8, 128), F32)
     r = got[...].reshape(NZ * NC, 128)
     r = jnp.concatenate([r] * 4, axis=0)
     keep = (iota((128, 128), 1) & 3) == (iota((128, 128), 0) >> 5)
@@ -291,11 +299,11 @@
         scratch_shapes=scratch,
         input_output_aliases={1: 0, 2: 1},
     )(early, in_vmem(up), in_vmem(head), *weights)
-    (send,) = pl.pallas_call(
+    send, _ = pl.pallas_call(
         regroup_kernel,
-        out_shape=(pltpu.VMEM((NX * NR, 8, 128), BF16),),
+        out_shape=(pltpu.VMEM((NX * NR, 8, 128), BF16), pltpu.VMEM((8, 128), F32)),
         in_specs=[vmem],
-        out_specs=(vmem,),
+        out_specs=(vmem, vmem),
     )(in_vmem(got))
     got = exchanged(send, plane_groups())
     return pl.pallas_call(

time: 39.3 us -> 36.6 us (0.931)
  the two profiles are of different devices: /device:TPU:128 before, /device:TPU:1 now
where the time goes in v5:
time: 36.6 us; the launch traced here: 36.3 us
  blocking collectives  19.2 us (52%)
  starting transfers between devices  8.72 us (24%)
  Pallas kernels  6.65 us (18%)
  waiting for transfers between devices  1.72 us (5%)
    all_to_all x1, blocking collectives, exchanged(): lax.all_to_all(value, EVERY, 0, 0, axis_index_groups=groups, tiled=True)  19.2 us
    all_to_all x1, starting transfers between devices, exchanged(): lax.all_to_all(value, EVERY, 0, 0, axis_index_groups=groups, tiled=True)  8.72 us
    pallas_call x1, Pallas kernels, on_device(): pl.pallas_call(slots_kernel, out_shape=(pltpu.VMEM((NZ * NC, 1, 128), F32...  3.74 us
    pallas_call x1, Pallas kernels, on_device(): pl.pallas_call(mask_kernel, out_shape=jax.ShapeDtypeStruct((4 * ROWS_T, 4...  2.05 us
    all_to_all x1, waiting for transfers between devices, exchanged(): lax.all_to_all(value, EVERY, 0, 0, axis_index_groups=groups, tiled=True)  1.72 us
    pallas_call x1, Pallas kernels, on_device(): pl.pallas_call(regroup_kernel, out_shape=(pltpu.VMEM((NX * NR, 8, 128), B...  0.78 us
  transfers between devices with their start and end apart: 1, of which 1 were waited for; matrix products, arithmetic and copies ran while one was open for 0% of the time, Pallas kernels for 0%

profile of v5, /device:TPU:1, one launch (start us, length us, event | category | flops | bytes accessed | tf_op | source)
XLA Modules:
  0.0 36.3 jit_solution(4570989685602414157)
XLA Ops:
  0.0 3.7 %shard_map.127 = (f32[32,1,128]{2,1,0:T(1,128)S(1)}, bf16[512,1024]{1,0:T(8,128)(2,1)S(1)}, bf16[32,256]{1,0:T(8,128)(2,1)S(1)}) custom-call(s32[1]{0:T(128)} %bitcast.early, s32[1,128]{1,0:T(1,128)} %bitcast.16, s32[1,128]{1,0:T(1,128)} %bitcast.17, s32[1,128]{1,0:T(1,128)} %bitcast.18, s32[2,128]{1,0:T(2,128)} %bitcast.15, s32[1,128]{1,0:T(1,128)} %bitcast.19, ...), custom_call_target="tpu_custom_call" | custom-call | tf_op jit(solution)/shard_map/pallas_call | solution.py:278
  3.8 19.2 %all_to_all.10.got = f32[32,1,128]{2,1,0:T(1,128)S(1)} all-to-all(f32[32,1,128]{2,1,0:T(1,128)S(1)} %get-tuple-element.11), channel_id=1, replica_groups={{68,64,76,72,84,80,92,88,100,96,108,104,116,112,124,120,4,0,12,8,20,16,..., dimensions={0} | all-to-all | bytes 32768 | tf_op jit(solution)/shard_map/all_to_all | solution.py:37
  22.9 0.8 %shard_map.128 = (bf16[16,8,128]{2,1,0:T(8,128)(2,1)}, f32[8,128]{1,0:T(8,128)}) custom-call(f32[32,1,128]{2,1,0:T(1,128)S(1)} %all_to_all.10.got), custom_call_target="tpu_custom_call" | custom-call | tf_op jit(solution)/shard_map/pallas_call | solution.py:302
  23.7 8.7 %all-to-all-start.1 = ((bf16[16,8,128]{2,1,0:T(8,128)(2,1)}), bf16[16,8,128]{2,1,0:T(8,128)(2,1)S(1)}, u32[]{:S(2)}, u32[]{:S(2)}) async-start(bf16[16,8,128]{2,1,0:T(8,128)(2,1)} %get-tuple-element.12), calls=%async_computation.1 | async-start | bytes 65536 | tf_op jit(solution)/shard_map/all_to_all | solution.py:37
  32.4 0.1 shard_map.129
  32.5 1.7 %all-to-all-done.1.got = bf16[16,8,128]{2,1,0:T(8,128)(2,1)S(1)} async-done(((bf16[16,8,128]{2,1,0:T(8,128)(2,1)}), bf16[16,8,128]{2,1,0:T(8,128)(2,1)S(1)}, u32[]{:S(2)}, u32[]{:S(2)}) %all-to-all-start.1) | async-done | bytes 32800 | tf_op jit(solution)/shard_map/all_to_all | solution.py:37
  34.2 2.1 %shard_map.130 = f32[64,256]{1,0:T(8,128)} custom-call(bf16[16,8,128]{2,1,0:T(8,128)(2,1)S(1)} %all-to-all-done.1.got, bf16[512,1024]{1,0:T(8,128)(2,1)S(1)} %get-tuple-element.15.up, bf16[32,256]{1,0:T(8,128)(2,1)S(1)} %get-tuple-element.16.head), custom_call_target="tpu_custom_call" | custom-call | tf_op jit(solution)/shard_map/pallas_call | solution.py:309
Async XLA Ops:
  23.7 10.5 %all-to-all-start.1 = ((bf16[16,8,128]{2,1,0:T(8,128)(2,1)}), bf16[16,8,128]{2,1,0:T(8,128)(2,1)S(1)}, u32[]{:S(2)}, u32[]{:S(2)}) async-start(bf16[16,8,128]{2,1,0:T(8,128)(2,1)} %get-tuple-element.12), calls=%async_computation.1 | async-start | bytes 65536 | tf_op jit(solution)/shard_map/all_to_all | solution.py:37

commit v6 on v5

--- a/solution.py
+++ b/solution.py
@@ -65,7 +65,7 @@
     return 0.5 * v * (1.0 + lax.erf(v * (1.0 / math.sqrt(2.0))))
 
 
-def local_tables(emb, one, two, pe, bias, w1, w2, w3, up_ref, head_ref):
+def local_tables(emb, one, two, pe, bias, w1, w2, w3, up_ref, head_ref, spread_ref):
     coord = (iota((16, P_DEV), 0).astype(F32) + 0.5) / (4.0 * CK) * 2.0 - 1.0
     angle_a = coord * pe[0:1, :] * (2.0 * math.pi)
     angle_b = coord * pe[1:2, :] * (2.0 * math.pi)
@@ -81,14 +81,14 @@
     hidden = jnp.maximum(nn(hidden, w2[...]), 0.0).astype(BF16)
     head_ref[...] = nt(w3[...], hidden).astype(BF16)
 
-    row = iota((16, P_DEV), 0)
-    x, y = row >> 2, row & 3
-    ahead = iota((16, P_DEV), 1) - (2 * (y & 1) + (x & 1)) * C2
-    pick = jnp.concatenate([(ahead == k).astype(F32) for k in range(C2)], axis=0).astype(BF16)
-    row = iota((16, 256), 0)
-    keep = (iota((16, 256), 1) >> 6) == 2 * ((row & 3) >> 1) + (row >> 3)
-    spread = nt(pick, jnp.concatenate([two[...]] * 4, axis=0))
-    wide = [jnp.where(keep, spread[16 * k : 16 * k + 16], 0.0) for k in range(C2)]
+    same = (iota((128, 128), 0) == iota((128, 128), 1)).astype(F32).astype(BF16)
+    turned = nt(same, jnp.concatenate([two[...]] * 4, axis=0))
+    off = iota((C2, 256), 1) >> 6
+    wide = []
+    for x in range(4):
+        for y in range(4):
+            e = 2 * (y & 1) + (x & 1)
+            wide.append(jnp.where(off == 2 * (y >> 1) + (x >> 1), turned[e * C2 : (e + 1) * C2], 0.0))
     wide = jnp.concatenate(wide, axis=0).astype(BF16)
     one_t = one[...].astype(F32).T.astype(BF16)
 
@@ -105,6 +105,11 @@
         up_ref[:, pl.ds(start, BLOCK)] = gelu(nn(wide, active)).astype(BF16)
         return carry
 
+    ahead = iota((EW, 256), 1) - 4 * iota((EW, 256), 0)
+    for x in range(4):
+        lanes = (ahead == x).astype(F32).astype(BF16)
+        spread_ref[x * 128 : x * 128 + 64, :] = lanes
+        spread_ref[x * 128 + 64 : x * 128 + 128, :] = lanes
     lax.fori_loop(0, CELLS // BLOCK, block, 0, unroll=UNROLL)
 
 
@@ -121,12 +126,11 @@
 
 
 def is_early():
-    at = [lax.axis_index(a) for a in EVERY]
-    return (at[1] <= 7) & (at[0] + at[1] + at[2] + at[3] > 0)
+    return lax.axis_index("z") <= 7
 
 
 def slots_kernel(early, tile, row, col, pts, conf, *rest):
-    weights, (send, up, head), scratch = rest[:8], rest[8:11], rest[11:]
+    weights, (send, *tables), scratch = rest[:8], rest[8:12], rest[12:]
     bufs, sems = scratch[:8], scratch[8]
     t = tile[...]
     names = (iota((P_DEV, P_DEV), 0) == t).astype(F32)
@@ -152,21 +156,12 @@
     @pl.when(early[0] == 1)
     def _():
         gathered_in(weights, bufs, sems)
-        local_tables(*bufs, up, head)
-
-
-def late_kernel(early, up_in, head_in, *rest):
-    weights, (up, head), scratch = rest[:8], rest[8:10], rest[10:]
+        local_tables(*bufs, *tables)
+
+
+def regroup_kernel(early, got, up_in, head_in, spread_in, *rest):
+    weights, (send, *tables), scratch = rest[:8], rest[8:12], rest[12:]
     bufs, sems = scratch[:8], scratch[8]
-
-    @pl.when(early[0] != 1)
-    def _():
-        gathered_in(weights, bufs, sems)
-        local_tables(*bufs, up, head)
-
-
-def regroup_kernel(got, send, spare):
-    spare[...] = jnp.zeros((8, 128), F32)
     r = got[...].reshape(NZ * NC, 128)
     r = jnp.concatenate([r] * 4, axis=0)
     keep = (iota((128, 128), 1) & 3) == (iota((128, 128), 0) >> 5)
@@ -179,33 +174,39 @@
         for j in range(NR):
             send[i * NR + j] = out[x * 8 : (x + 1) * 8, :].astype(BF16)
 
-
-def mask_kernel(got, up, head, out):
+    @pl.when(early[0] != 1)
+    def _():
+        gathered_in(weights, bufs, sems)
+        local_tables(*bufs, *tables)
+
+
+def mask_kernel(got, up, head, spread, out):
     lane = iota((8, 128), 1)
     own, below = [], []
     for j in range(8):
         a, b = got[j].astype(F32), got[j + 8].astype(F32)
         own.append(jnp.where(lane < 64, a, pltpu.roll(b, 64, 1)))
         below.append(jnp.where(lane < 64, pltpu.roll(a, 64, 1), b))
-    own, below = jnp.concatenate(own, axis=1), jnp.concatenate(below, axis=1)
+    own, below = (jnp.concatenate(v, axis=1).astype(BF16) for v in (own, below))
     many = 1024
-    r_at = iota((16, many), 0).astype(F32)
-    c_at = iota((EW, many), 0).astype(F32)
-    table = head[...]
+    c_at = iota((EW, many), 0).astype(F32).astype(BF16)
+    r_at = c_at[:16]
+    zero, unit = BF16(0.0), BF16(1.0)
+    blank = jnp.zeros((EW, many), BF16)
 
     def one_hot(v, at):
-        return (at == v).astype(BF16)
+        return jnp.maximum(unit - jnp.abs(at - v), zero)
+
+    def window(v, at):
+        return jnp.clip(BF16(2.5) - jnp.abs(at - (v + BF16(1.5))), zero, unit)
 
     def factors(v, rows):
         row, col, conf, first, second = (v[i : i + 1, :] for i in range(5))
-        hot_a, hot_b = one_hot(first, r_at), one_hot(second, r_at)
-        hot = jnp.concatenate([hot_a[i : i + 1, :] * hot_b for i in range(16)], axis=0)
-        heads = nn(table, hot).astype(BF16)
-        d = r_at - row
-        in_row = ((d >= 0.0) & (d <= 3.0)).astype(BF16)
-        d = c_at - col
-        in_col = jnp.where((d >= 0.0) & (d <= 3.0), conf, 0.0).astype(BF16)
-        blank = jnp.zeros((EW, many), BF16)
+        ahead = r_at - (BF16(16.0) * first + second)
+        hot = [jnp.where(ahead == BF16(-16.0 * i), unit, zero) for i in range(16)]
+        hot = jnp.concatenate(hot, axis=0)
+        heads = nn(head[...], hot).astype(BF16)
+        in_row, in_col = window(row, r_at), window(col, c_at) * conf
         even, odd = jnp.concatenate([in_col, blank], axis=0), jnp.concatenate([blank, in_col], axis=0)
         lefts = [heads * in_row[i : i + 1, :] for i in range(rows)]
         return (
@@ -214,33 +215,27 @@
         )
 
     total = factors(own, 16)
-    spill = factors(below, 4)
-    total = jnp.concatenate([total[:64] + spill, total[64:]], axis=0)
-
-    sub = iota((8, 128), 0)
-    mine = (sub >> 2) == (iota((8, 128), 1) >> 6)
+    total = jnp.concatenate([total[:64] + factors(below, 4), total[64:]], axis=0)
+    total = (total * 0.25).astype(BF16)
+
+    at, lane = iota((32, 256), 0), iota((32, 256), 1)
+    gather = ((lane >> 4) == 4 * (at >> 3) + (at & 3)).astype(F32).astype(BF16)
+    mine = (iota((32, 256), 0) >> 2 & 1) == (iota((32, 256), 1) >> 6 & 1)
     blocks = []
-    for j in range(8):
-        h = total[j * 32 : (j + 1) * 32, :]
-        low, high = jnp.zeros((8, 128), F32), jnp.zeros((8, 128), F32)
-        for k in range(C2):
-            u = up[k * 16 : (k + 1) * 16, j * 128 : (j + 1) * 128].astype(F32)
-            w = h[k : k + 1, :]
-            low, high = low + u[:8] * w, high + u[8:] * w
-        pieces = []
-        for v in (low, high):
-            turned = pltpu.roll(v, 4, 0)
-            pieces.append(jnp.where(mine, jnp.where(sub < 4, v, turned), 0.0))
-            pieces.append(jnp.where(mine, jnp.where(sub < 4, turned, v), 0.0))
-        blocks.append(jnp.concatenate(pieces, axis=1))
-    flat = jnp.concatenate(blocks, axis=0) * 0.25
-    at, lane = iota((512, 256), 0), iota((512, 256), 1)
-    spread = (lane == 4 * (at & 63) + (at >> 7)).astype(BF16)
+    for j in range(0, 8, 2):
+        cells = slice(j * 128, (j + 2) * 128)
+        h = jnp.concatenate([total[(j + i) * 32 : (j + i + 1) * 32, :] for i in range(2)], axis=1)
+        terms = [up[q * C2 : (q + 1) * C2, cells] * h for q in range(16)]
+        terms = [t[:16] + t[16:] for t in terms]
+        sums = jnp.where(mine, nn(gather, jnp.concatenate(terms, axis=0)), 0.0)
+        for i in range(2):
+            part = sums[:, i * 128 : (i + 1) * 128]
+            blocks.append(jnp.concatenate([part[8 * x : 8 * x + 8] for x in range(NX)], axis=1))
+    flat = jnp.concatenate(blocks, axis=0)
     top = flat.astype(BF16)
-    rest = flat - top.astype(F32)
-    mid = rest.astype(BF16)
-    last = (rest - mid.astype(F32)).astype(BF16)
-    out[...] = nn(top, spread) + (nn(mid, spread) + nn(last, spread))
+    rest = (flat - top.astype(F32)).astype(BF16)
+    both = nn(jnp.concatenate([top, rest], axis=0), spread[...])
+    out[...] = both[:64] + both[64:]
 
 
 def on_device(
@@ -274,12 +269,13 @@
     )
     up_shape = pltpu.VMEM((16 * C2, CELLS), BF16)
     head_shape = pltpu.VMEM((C2, 256), BF16)
+    tables = (up_shape, head_shape, pltpu.VMEM((512, 256), BF16))
     scratch = [pltpu.VMEM(w.shape, w.dtype) for w in weights] + [pltpu.SemaphoreType.DMA((8,))]
-    send, up, head = pl.pallas_call(
+    send, *made = pl.pallas_call(
         slots_kernel,
-        out_shape=(pltpu.VMEM((NZ * NC, 1, 128), F32), up_shape, head_shape),
+        out_shape=(pltpu.VMEM((NZ * NC, 1, 128), F32), *tables),
         in_specs=[smem] + [vmem] * 5 + [hbm] * 8,
-        out_specs=(vmem, vmem, vmem),
+        out_specs=(vmem,) * 4,
         scratch_shapes=scratch,
     )(
         early,
@@ -291,27 +287,21 @@
         *weights,
     )
     got = exchanged(send, column_groups())
-    up, head = pl.pallas_call(
-        late_kernel,
-        out_shape=(up_shape, head_shape),
-        in_specs=[smem] + [vmem] * 2 + [hbm] * 8,
-        out_specs=(vmem, vmem),
+    send, *made = pl.pallas_call(
+        regroup_kernel,
+        out_shape=(pltpu.VMEM((NX * NR, 8, 128), BF16), *tables),
+        in_specs=[smem] + [vmem] * 4 + [hbm] * 8,
+        out_specs=(vmem,) * 4,
         scratch_shapes=scratch,
-        input_output_aliases={1: 0, 2: 1},
-    )(early, in_vmem(up), in_vmem(head), *weights)
-    send, _ = pl.pallas_call(
-        regroup_kernel,
-        out_shape=(pltpu.VMEM((NX * NR, 8, 128), BF16), pltpu.VMEM((8, 128), F32)),
-        in_specs=[vmem],
-        out_specs=(vmem, vmem),
-    )(in_vmem(got))
+        input_output_aliases={2: 1, 3: 2, 4: 3},
+    )(early, in_vmem(got), *map(in_vmem, made), *weights)
     got = exchanged(send, plane_groups())
     return pl.pallas_call(
         mask_kernel,
         out_shape=jax.ShapeDtypeStruct((4 * ROWS_T, 4 * EW), F32),
-        in_specs=[vmem] * 3,
+        in_specs=[vmem] * 4,
         out_specs=vmem,
-    )(in_vmem(got), in_vmem(up), in_vmem(head))
+    )(in_vmem(got), *map(in_vmem, made))
 
 
 def solution(mesh):

time: 36.6 us -> 35.7 us (0.975)
  blocking collectives: 19.2 us -> 29 us
  starting transfers between devices: 8.72 us -> 0 us
  waiting for transfers between devices: 1.72 us -> 0 us
  Pallas kernels: 6.65 us -> 6.16 us
    all_to_all x1 -> x2, blocking collectives: 19.2 us -> 29 us  [exchanged(): lax.all_to_all(value, EVERY, 0, 0, axis_index_groups=groups, tiled=True)]
    all_to_all x1 -> x0, starting transfers between devices: 8.72 us -> none  [exchanged(): lax.all_to_all(value, EVERY, 0, 0, axis_index_groups=groups, tiled=True)]
    all_to_all x1 -> x0, waiting for transfers between devices: 1.72 us -> none  [exchanged(): lax.all_to_all(value, EVERY, 0, 0, axis_index_groups=groups, tiled=True)]
    pallas_call x1, Pallas kernels: 0.78 us -> 0.23 us  [on_device(): pl.pallas_call(regroup_kernel, out_shape=(pltpu.VMEM((NX * NR, 8, 128), B...]
  transfers between devices with their start and end apart: 1 -> 0, of which waited for: 1 -> 0; matrix products, arithmetic and copies ran while one was open for 0% -> 0% of each run, Pallas kernels for 0% -> 0%
where the time goes in v6:
time: 35.7 us; the launch traced here: 35.1 us
  blocking collectives  29 us (81%)
  Pallas kernels  6.16 us (17%)
    all_to_all x2, blocking collectives, exchanged(): lax.all_to_all(value, EVERY, 0, 0, axis_index_groups=groups, tiled=True)  29 us
    pallas_call x1, Pallas kernels, on_device(): pl.pallas_call(slots_kernel, out_shape=(pltpu.VMEM((NZ * NC, 1, 128), F32...  3.89 us
    pallas_call x1, Pallas kernels, on_device(): pl.pallas_call(mask_kernel, out_shape=jax.ShapeDtypeStruct((4 * ROWS_T, 4...  2.03 us

profile of v6, /device:TPU:1, one launch (start us, length us, event | category | flops | bytes accessed | tf_op | source)
XLA Modules:
  0.0 35.1 jit_solution(6546639461907603742)
XLA Ops:
  0.0 3.9 %shard_map.127 = (f32[32,1,128]{2,1,0:T(1,128)S(1)}, bf16[512,1024]{1,0:T(8,128)(2,1)S(1)}, bf16[32,256]{1,0:T(8,128)(2,1)S(1)}, bf16[512,256]{1,0:T(8,128)(2,1)S(1)}) custom-call(s32[1]{0:T(128)} %bitcast.early, s32[1,128]{1,0:T(1,128)} %bitcast.16, s32[1,128]{1,0:T(1,128)} %bitcast.17, s32[1,128]{1,0:T(1,128)} %bitcast.18, s32[2,128]{1,0:T(2,128)} %bitcast.15, ...), custom_call_target="tpu_custom_call" | custom-call | tf_op jit(solution)/shard_map/pallas_call | solution.py:274
  3.9 20.4 %all_to_all.10.got = f32[32,1,128]{2,1,0:T(1,128)S(1)} all-to-all(f32[32,1,128]{2,1,0:T(1,128)S(1)} %get-tuple-element.13), channel_id=1, replica_groups={{68,64,76,72,84,80,92,88,100,96,108,104,116,112,124,120,4,0,12,8,20,16,..., dimensions={0} | all-to-all | bytes 32768 | tf_op jit(solution)/shard_map/all_to_all | solution.py:37
  24.3 0.2 shard_map.128
  24.5 8.6 %all_to_all.11.got = bf16[16,8,128]{2,1,0:T(8,128)(2,1)S(1)} all-to-all(bf16[16,8,128]{2,1,0:T(8,128)(2,1)S(1)} %get-tuple-element.17), channel_id=1, replica_groups={{258,259,256,257,386,387,384,385,2,3,0,1,130,131,128,129},{262,263,260,..., dimensions={0} | all-to-all | bytes 65536 | tf_op jit(solution)/shard_map/all_to_all | solution.py:37
  33.1 2.0 %shard_map.129 = f32[64,256]{1,0:T(8,128)} custom-call(bf16[16,8,128]{2,1,0:T(8,128)(2,1)S(1)} %all_to_all.11.got, bf16[512,1024]{1,0:T(8,128)(2,1)S(1)} %get-tuple-element.18.up, bf16[32,256]{1,0:T(8,128)(2,1)S(1)} %get-tuple-element.19.head, bf16[512,256]{1,0:T(8,128)(2,1)S(1)} %get-tuple-element.20.spread), custom_call_target="tpu_custom_call" | custom-call | tf_op jit(solution)/shard_map/pallas_call | solution.py:299

commit v7 on v6

--- a/solution.py
+++ b/solution.py
@@ -81,14 +81,14 @@
     hidden = jnp.maximum(nn(hidden, w2[...]), 0.0).astype(BF16)
     head_ref[...] = nt(w3[...], hidden).astype(BF16)
 
-    same = (iota((128, 128), 0) == iota((128, 128), 1)).astype(F32).astype(BF16)
-    turned = nt(same, jnp.concatenate([two[...]] * 4, axis=0))
-    off = iota((C2, 256), 1) >> 6
-    wide = []
-    for x in range(4):
-        for y in range(4):
-            e = 2 * (y & 1) + (x & 1)
-            wide.append(jnp.where(off == 2 * (y >> 1) + (x >> 1), turned[e * C2 : (e + 1) * C2], 0.0))
+    row = iota((16, P_DEV), 0)
+    x, y = row >> 2, row & 3
+    ahead = iota((16, P_DEV), 1) - (2 * (y & 1) + (x & 1)) * C2
+    pick = jnp.concatenate([(ahead == k).astype(F32) for k in range(C2)], axis=0).astype(BF16)
+    row = iota((16, 256), 0)
+    keep = (iota((16, 256), 1) >> 6) == 2 * ((row & 3) >> 1) + (row >> 3)
+    spread = nt(pick, jnp.concatenate([two[...]] * 4, axis=0))
+    wide = [jnp.where(keep, spread[16 * k : 16 * k + 16], 0.0) for k in range(C2)]
     wide = jnp.concatenate(wide, axis=0).astype(BF16)
     one_t = one[...].astype(F32).T.astype(BF16)
 
@@ -192,10 +192,7 @@
     c_at = iota((EW, many), 0).astype(F32).astype(BF16)
     r_at = c_at[:16]
     zero, unit = BF16(0.0), BF16(1.0)
-    blank = jnp.zeros((EW, many), BF16)
-
-    def one_hot(v, at):
-        return jnp.maximum(unit - jnp.abs(at - v), zero)
+    left = iota((C2, 128), 1) < 64
 
     def window(v, at):
         return jnp.clip(BF16(2.5) - jnp.abs(at - (v + BF16(1.5))), zero, unit)
@@ -207,30 +204,33 @@
         hot = jnp.concatenate(hot, axis=0)
         heads = nn(head[...], hot).astype(BF16)
         in_row, in_col = window(row, r_at), window(col, c_at) * conf
-        even, odd = jnp.concatenate([in_col, blank], axis=0), jnp.concatenate([blank, in_col], axis=0)
+        in_col = jnp.concatenate([in_col, in_col], axis=0)
         lefts = [heads * in_row[i : i + 1, :] for i in range(rows)]
-        return (
-            nt(jnp.concatenate(lefts[0::2], axis=0), even)
-            + nt(jnp.concatenate(lefts[1::2], axis=0), odd)
-        )
+        half = max(rows // 2, 4)
+        sums = [nt(jnp.concatenate(lefts[i : i + half], axis=0), in_col) for i in range(0, rows, half)]
+        sums = jnp.concatenate(sums, axis=0)
+        sums = [jnp.where(left, sums[i : i + 32], sums[i + 32 : i + 64]) for i in range(0, 32 * rows, 64)]
+        return jnp.concatenate(sums, axis=0)
 
     total = factors(own, 16)
     total = jnp.concatenate([total[:64] + factors(below, 4), total[64:]], axis=0)
-    total = (total * 0.25).astype(BF16)
-
-    at, lane = iota((32, 256), 0), iota((32, 256), 1)
-    gather = ((lane >> 4) == 4 * (at >> 3) + (at & 3)).astype(F32).astype(BF16)
-    mine = (iota((32, 256), 0) >> 2 & 1) == (iota((32, 256), 1) >> 6 & 1)
+    total = total * 0.25
+
+    sub = iota((8, 128), 0)
+    mine = (sub >> 2) == (iota((8, 128), 1) >> 6)
     blocks = []
-    for j in range(0, 8, 2):
-        cells = slice(j * 128, (j + 2) * 128)
-        h = jnp.concatenate([total[(j + i) * 32 : (j + i + 1) * 32, :] for i in range(2)], axis=1)
-        terms = [up[q * C2 : (q + 1) * C2, cells] * h for q in range(16)]
-        terms = [t[:16] + t[16:] for t in terms]
-        sums = jnp.where(mine, nn(gather, jnp.concatenate(terms, axis=0)), 0.0)
-        for i in range(2):
-            part = sums[:, i * 128 : (i + 1) * 128]
-            blocks.append(jnp.concatenate([part[8 * x : 8 * x + 8] for x in range(NX)], axis=1))
+    for j in range(8):
+        cells = slice(j * 128, (j + 1) * 128)
+        h = total[j * 32 : (j + 1) * 32, :]
+        terms = [up[k * 16 : (k + 1) * 16, cells].astype(F32) * h[k : k + 1, :] for k in range(C2)]
+        while len(terms) > 1:
+            terms = [a + b for a, b in zip(terms[0::2], terms[1::2])]
+        pieces = []
+        for v in (terms[0][:8], terms[0][8:]):
+            turned = pltpu.roll(v, 4, 0)
+            pieces.append(jnp.where(mine, jnp.where(sub < 4, v, turned), 0.0))
+            pieces.append(jnp.where(mine, jnp.where(sub < 4, turned, v), 0.0))
+        blocks.append(jnp.concatenate(pieces, axis=1))
     flat = jnp.concatenate(blocks, axis=0)
     top = flat.astype(BF16)
     rest = (flat - top.astype(F32)).astype(BF16)

time: 35.7 us -> 35.5 us (level)
  Pallas kernels: 6.16 us -> 5.77 us
where the time goes in v7:
time: 35.5 us; the launch traced here: 34.9 us
  blocking collectives  29.1 us (82%)
  Pallas kernels  5.77 us (16%)
    all_to_all x2, blocking collectives, exchanged(): lax.all_to_all(value, EVERY, 0, 0, axis_index_groups=groups, tiled=True)  29.1 us
    pallas_call x1, Pallas kernels, on_device(): pl.pallas_call(slots_kernel, out_shape=(pltpu.VMEM((NZ * NC, 1, 128), F32...  3.75 us
    pallas_call x1, Pallas kernels, on_device(): pl.pallas_call(mask_kernel, out_shape=jax.ShapeDtypeStruct((4 * ROWS_T, 4...  1.78 us

profile of v7, /device:TPU:1, one launch (start us, length us, event | category | flops | bytes accessed | tf_op | source)
XLA Modules:
  0.0 34.9 jit_solution(8521519372692067513)
XLA Ops:
  0.0 3.7 %shard_map.127 = (f32[32,1,128]{2,1,0:T(1,128)S(1)}, bf16[512,1024]{1,0:T(8,128)(2,1)S(1)}, bf16[32,256]{1,0:T(8,128)(2,1)S(1)}, bf16[512,256]{1,0:T(8,128)(2,1)S(1)}) custom-call(s32[1]{0:T(128)} %bitcast.early, s32[1,128]{1,0:T(1,128)} %bitcast.16, s32[1,128]{1,0:T(1,128)} %bitcast.17, s32[1,128]{1,0:T(1,128)} %bitcast.18, s32[2,128]{1,0:T(2,128)} %bitcast.15, ...), custom_call_target="tpu_custom_call" | custom-call | tf_op jit(solution)/shard_map/pallas_call | solution.py:274
  3.8 20.4 %all_to_all.10.got = f32[32,1,128]{2,1,0:T(1,128)S(1)} all-to-all(f32[32,1,128]{2,1,0:T(1,128)S(1)} %get-tuple-element.13), channel_id=1, replica_groups={{68,64,76,72,84,80,92,88,100,96,108,104,116,112,124,120,4,0,12,8,20,16,..., dimensions={0} | all-to-all | bytes 32768 | tf_op jit(solution)/shard_map/all_to_all | solution.py:37
  24.1 0.2 shard_map.128
  24.4 8.8 %all_to_all.11.got = bf16[16,8,128]{2,1,0:T(8,128)(2,1)S(1)} all-to-all(bf16[16,8,128]{2,1,0:T(8,128)(2,1)S(1)} %get-tuple-element.17), channel_id=1, replica_groups={{258,259,256,257,386,387,384,385,2,3,0,1,130,131,128,129},{262,263,260,..., dimensions={0} | all-to-all | bytes 65536 | tf_op jit(solution)/shard_map/all_to_all | solution.py:37
  33.1 1.8 %shard_map.129 = f32[64,256]{1,0:T(8,128)} custom-call(bf16[16,8,128]{2,1,0:T(8,128)(2,1)S(1)} %all_to_all.11.got, bf16[512,1024]{1,0:T(8,128)(2,1)S(1)} %get-tuple-element.18.up, bf16[32,256]{1,0:T(8,128)(2,1)S(1)} %get-tuple-element.19.head, bf16[512,256]{1,0:T(8,128)(2,1)S(1)} %get-tuple-element.20.spread), custom_call_target="tpu_custom_call" | custom-call | tf_op jit(solution)/shard_map/pallas_call | solution.py:299

commit v8 on v7

--- a/solution.py
+++ b/solution.py
@@ -17,7 +17,7 @@
 P_DEV = 128
 NX, NZ, NC, NR = 4, 16, 2, 4
 CELLS = ROWS_T * EW
-Z_FIRST, C_FIRST, X_FIRST, R_FIRST = 8, 1, 2, 2
+Z_FIRST, C_FIRST, X_FIRST, R_FIRST = 9, 1, 2, 2
 UNROLL, BLOCK = 4, 256
 EVERY = ("x", "z", "core", "rep")
 F32 = jnp.float32

time: 35.5 us -> 35.5 us (level)
  no operation moved by 1% of the time
where the time goes in v8:
time: 35.5 us; the launch traced here: 34.9 us
  blocking collectives  29.1 us (82%)
  Pallas kernels  5.76 us (16%)
    all_to_all x2, blocking collectives, exchanged(): lax.all_to_all(value, EVERY, 0, 0, axis_index_groups=groups, tiled=True)  29.1 us
    pallas_call x1, Pallas kernels, on_device(): pl.pallas_call(slots_kernel, out_shape=(pltpu.VMEM((NZ * NC, 1, 128), F32...  3.75 us
    pallas_call x1, Pallas kernels, on_device(): pl.pallas_call(mask_kernel, out_shape=jax.ShapeDtypeStruct((4 * ROWS_T, 4...  1.78 us

profile of v8, /device:TPU:1, one launch (start us, length us, event | category | flops | bytes accessed | tf_op | source)
XLA Modules:
  0.0 34.9 jit_solution(17704014514275185534)
XLA Ops:
  0.0 3.7 %shard_map.127 = (f32[32,1,128]{2,1,0:T(1,128)S(1)}, bf16[512,1024]{1,0:T(8,128)(2,1)S(1)}, bf16[32,256]{1,0:T(8,128)(2,1)S(1)}, bf16[512,256]{1,0:T(8,128)(2,1)S(1)}) custom-call(s32[1]{0:T(128)} %bitcast.early, s32[1,128]{1,0:T(1,128)} %bitcast.16, s32[1,128]{1,0:T(1,128)} %bitcast.17, s32[1,128]{1,0:T(1,128)} %bitcast.18, s32[2,128]{1,0:T(2,128)} %bitcast.15, ...), custom_call_target="tpu_custom_call" | custom-call | tf_op jit(solution)/shard_map/pallas_call | solution.py:274
  3.8 20.4 %all_to_all.10.got = f32[32,1,128]{2,1,0:T(1,128)S(1)} all-to-all(f32[32,1,128]{2,1,0:T(1,128)S(1)} %get-tuple-element.13), channel_id=1, replica_groups={{76,72,84,80,92,88,100,96,108,104,116,112,124,120,4,0,12,8,20,16,28,24,..., dimensions={0} | all-to-all | bytes 32768 | tf_op jit(solution)/shard_map/all_to_all | solution.py:37
  24.1 0.2 shard_map.128
  24.3 8.8 %all_to_all.11.got = bf16[16,8,128]{2,1,0:T(8,128)(2,1)S(1)} all-to-all(bf16[16,8,128]{2,1,0:T(8,128)(2,1)S(1)} %get-tuple-element.17), channel_id=1, replica_groups={{258,259,256,257,386,387,384,385,2,3,0,1,130,131,128,129},{262,263,260,..., dimensions={0} | all-to-all | bytes 65536 | tf_op jit(solution)/shard_map/all_to_all | solution.py:37
  33.1 1.8 %shard_map.129 = f32[64,256]{1,0:T(8,128)} custom-call(bf16[16,8,128]{2,1,0:T(8,128)(2,1)S(1)} %all_to_all.11.got, bf16[512,1024]{1,0:T(8,128)(2,1)S(1)} %get-tuple-element.18.up, bf16[32,256]{1,0:T(8,128)(2,1)S(1)} %get-tuple-element.19.head, bf16[512,256]{1,0:T(8,128)(2,1)S(1)} %get-tuple-element.20.spread), custom_call_target="tpu_custom_call" | custom-call | tf_op jit(solution)/shard_map/pallas_call | solution.py:299

commit v9 on v8

--- a/solution.py
+++ b/solution.py
@@ -129,7 +129,7 @@
     return lax.axis_index("z") <= 7
 
 
-def slots_kernel(early, tile, row, col, pts, conf, *rest):
+def slots_kernel(tile, row, col, pts, conf, *rest):
     weights, (send, *tables), scratch = rest[:8], rest[8:12], rest[12:]
     bufs, sems = scratch[:8], scratch[8]
     t = tile[...]
@@ -153,13 +153,13 @@
     out = part(t, rank, values) + part(t + 1, rank + 2, [values[0] - ROWS_T] + values[1:])
     send[...] = out.reshape(NZ * NC, 1, 128)
 
-    @pl.when(early[0] == 1)
+    @pl.when(is_early())
     def _():
         gathered_in(weights, bufs, sems)
         local_tables(*bufs, *tables)
 
 
-def regroup_kernel(early, got, up_in, head_in, spread_in, *rest):
+def regroup_kernel(got, up_in, head_in, spread_in, *rest):
     weights, (send, *tables), scratch = rest[:8], rest[8:12], rest[12:]
     bufs, sems = scratch[:8], scratch[8]
     r = got[...].reshape(NZ * NC, 128)
@@ -174,7 +174,7 @@
         for j in range(NR):
             send[i * NR + j] = out[x * 8 : (x + 1) * 8, :].astype(BF16)
 
-    @pl.when(early[0] != 1)
+    @pl.when(jnp.logical_not(is_early()))
     def _():
         gathered_in(weights, bufs, sems)
         local_tables(*bufs, *tables)
@@ -253,8 +253,6 @@
     conv_one,
     conv_two,
 ):
-    early = is_early().astype(I32).reshape(1)
-    smem = pl.BlockSpec(memory_space=pltpu.SMEM)
     vmem = pl.BlockSpec(memory_space=pltpu.VMEM)
     hbm = pl.BlockSpec(memory_space=pl.ANY)
     weights = (
@@ -274,11 +272,10 @@
     send, *made = pl.pallas_call(
         slots_kernel,
         out_shape=(pltpu.VMEM((NZ * NC, 1, 128), F32), *tables),
-        in_specs=[smem] + [vmem] * 5 + [hbm] * 8,
+        in_specs=[vmem] * 5 + [hbm] * 8,
         out_specs=(vmem,) * 4,
         scratch_shapes=scratch,
     )(
-        early,
         prompt_tile.reshape(1, P_DEV),
         crop_row.reshape(1, P_DEV),
         crop_col.reshape(1, P_DEV),
@@ -290,11 +287,11 @@
     send, *made = pl.pallas_call(
         regroup_kernel,
         out_shape=(pltpu.VMEM((NX * NR, 8, 128), BF16), *tables),
-        in_specs=[smem] + [vmem] * 4 + [hbm] * 8,
+        in_specs=[vmem] * 4 + [hbm] * 8,
         out_specs=(vmem,) * 4,
         scratch_shapes=scratch,
-        input_output_aliases={2: 1, 3: 2, 4: 3},
-    )(early, in_vmem(got), *map(in_vmem, made), *weights)
+        input_output_aliases={1: 1, 2: 2, 3: 3},
+    )(in_vmem(got), *map(in_vmem, made), *weights)
     got = exchanged(send, plane_groups())
     return pl.pallas_call(
         mask_kernel,

time: 35.5 us -> 35.5 us (level)
  no operation moved by 1% of the time
where the time goes in v9:
time: 35.5 us; the launch traced here: 34.9 us
  blocking collectives  29.1 us (82%)
  Pallas kernels  5.76 us (16%)
    all_to_all x2, blocking collectives, exchanged(): lax.all_to_all(value, EVERY, 0, 0, axis_index_groups=groups, tiled=True)  29.1 us
    pallas_call x1, Pallas kernels, on_device(): pl.pallas_call(slots_kernel, out_shape=(pltpu.VMEM((NZ * NC, 1, 128), F32...  3.75 us
    pallas_call x1, Pallas kernels, on_device(): pl.pallas_call(mask_kernel, out_shape=jax.ShapeDtypeStruct((4 * ROWS_T, 4...  1.78 us

profile of v9, /device:TPU:1, one launch (start us, length us, event | category | flops | bytes accessed | tf_op | source)
XLA Modules:
  0.0 34.9 jit_solution(2973977694221111175)
XLA Ops:
  0.0 3.7 %shard_map.127 = (f32[32,1,128]{2,1,0:T(1,128)S(1)}, bf16[512,1024]{1,0:T(8,128)(2,1)S(1)}, bf16[32,256]{1,0:T(8,128)(2,1)S(1)}, bf16[512,256]{1,0:T(8,128)(2,1)S(1)}) custom-call(s32[1,128]{1,0:T(1,128)} %bitcast.15, s32[1,128]{1,0:T(1,128)} %bitcast.16, s32[1,128]{1,0:T(1,128)} %bitcast.17, s32[2,128]{1,0:T(2,128)} %bitcast.14, s32[1,128]{1,0:T(1,128)} %bitcast.18, ...), custom_call_target="tpu_custom_call" | custom-call | tf_op jit(solution)/shard_map/pallas_call | solution.py:272
  3.8 20.4 %all_to_all.10.got = f32[32,1,128]{2,1,0:T(1,128)S(1)} all-to-all(f32[32,1,128]{2,1,0:T(1,128)S(1)} %get-tuple-element.13), channel_id=1, replica_groups={{76,72,84,80,92,88,100,96,108,104,116,112,124,120,4,0,12,8,20,16,28,24,..., dimensions={0} | all-to-all | bytes 32768 | tf_op jit(solution)/shard_map/all_to_all | solution.py:37
  24.1 0.2 shard_map.128
  24.3 8.8 %all_to_all.11.got = bf16[16,8,128]{2,1,0:T(8,128)(2,1)S(1)} all-to-all(bf16[16,8,128]{2,1,0:T(8,128)(2,1)S(1)} %get-tuple-element.17), channel_id=1, replica_groups={{258,259,256,257,386,387,384,385,2,3,0,1,130,131,128,129},{262,263,260,..., dimensions={0} | all-to-all | bytes 65536 | tf_op jit(solution)/shard_map/all_to_all | solution.py:37
  33.1 1.8 %shard_map.129 = f32[64,256]{1,0:T(8,128)} custom-call(bf16[16,8,128]{2,1,0:T(8,128)(2,1)S(1)} %all_to_all.11.got, bf16[512,1024]{1,0:T(8,128)(2,1)S(1)} %get-tuple-element.18.up, bf16[32,256]{1,0:T(8,128)(2,1)S(1)} %get-tuple-element.19.head, bf16[512,256]{1,0:T(8,128)(2,1)S(1)} %get-tuple-element.20.spread), custom_call_target="tpu_custom_call" | custom-call | tf_op jit(solution)/shard_map/pallas_call | solution.py:296

commit v10 on v9

--- a/solution.py
+++ b/solution.py
@@ -17,7 +17,7 @@
 P_DEV = 128
 NX, NZ, NC, NR = 4, 16, 2, 4
 CELLS = ROWS_T * EW
-Z_FIRST, C_FIRST, X_FIRST, R_FIRST = 9, 1, 2, 2
+Z_FIRST, C_FIRST, X_FIRST, R_FIRST = 11, 1, 2, 2
 UNROLL, BLOCK = 4, 256
 EVERY = ("x", "z", "core", "rep")
 F32 = jnp.float32
@@ -126,7 +126,7 @@
 
 
 def is_early():
-    return lax.axis_index("z") <= 7
+    return lax.axis_index("z") <= 5
 
 
 def slots_kernel(tile, row, col, pts, conf, *rest):

time: 35.5 us -> 36.2 us (1.020)
  blocking collectives: 29.1 us -> 29.9 us
    all_to_all x2, blocking collectives: 29.1 us -> 29.9 us  [exchanged(): lax.all_to_all(value, EVERY, 0, 0, axis_index_groups=groups, tiled=True)]
where the time goes in v10:
time: 36.2 us; the launch traced here: 35.7 us
  blocking collectives  29.9 us (83%)
  Pallas kernels  5.77 us (16%)
    all_to_all x2, blocking collectives, exchanged(): lax.all_to_all(value, EVERY, 0, 0, axis_index_groups=groups, tiled=True)  29.9 us
    pallas_call x1, Pallas kernels, on_device(): pl.pallas_call(slots_kernel, out_shape=(pltpu.VMEM((NZ * NC, 1, 128), F32...  3.75 us
    pallas_call x1, Pallas kernels, on_device(): pl.pallas_call(mask_kernel, out_shape=jax.ShapeDtypeStruct((4 * ROWS_T, 4...  1.78 us

profile of v10, /device:TPU:1, one launch (start us, length us, event | category | flops | bytes accessed | tf_op | source)
XLA Modules:
  0.0 35.7 jit_solution(5155430033204955653)
XLA Ops:
  0.0 3.7 %shard_map.127 = (f32[32,1,128]{2,1,0:T(1,128)S(1)}, bf16[512,1024]{1,0:T(8,128)(2,1)S(1)}, bf16[32,256]{1,0:T(8,128)(2,1)S(1)}, bf16[512,256]{1,0:T(8,128)(2,1)S(1)}) custom-call(s32[1,128]{1,0:T(1,128)} %bitcast.15, s32[1,128]{1,0:T(1,128)} %bitcast.16, s32[1,128]{1,0:T(1,128)} %bitcast.17, s32[2,128]{1,0:T(2,128)} %bitcast.14, s32[1,128]{1,0:T(1,128)} %bitcast.18, ...), custom_call_target="tpu_custom_call" | custom-call | tf_op jit(solution)/shard_map/pallas_call | solution.py:272
  3.8 20.4 %all_to_all.10.got = f32[32,1,128]{2,1,0:T(1,128)S(1)} all-to-all(f32[32,1,128]{2,1,0:T(1,128)S(1)} %get-tuple-element.13), channel_id=1, replica_groups={{92,88,100,96,108,104,116,112,124,120,4,0,12,8,20,16,28,24,36,32,44,40,..., dimensions={0} | all-to-all | bytes 32768 | tf_op jit(solution)/shard_map/all_to_all | solution.py:37
  24.1 0.2 shard_map.128
  24.4 9.5 %all_to_all.11.got = bf16[16,8,128]{2,1,0:T(8,128)(2,1)S(1)} all-to-all(bf16[16,8,128]{2,1,0:T(8,128)(2,1)S(1)} %get-tuple-element.17), channel_id=1, replica_groups={{258,259,256,257,386,387,384,385,2,3,0,1,130,131,128,129},{262,263,260,..., dimensions={0} | all-to-all | bytes 65536 | tf_op jit(solution)/shard_map/all_to_all | solution.py:37
  33.9 1.8 %shard_map.129 = f32[64,256]{1,0:T(8,128)} custom-call(bf16[16,8,128]{2,1,0:T(8,128)(2,1)S(1)} %all_to_all.11.got, bf16[512,1024]{1,0:T(8,128)(2,1)S(1)} %get-tuple-element.18.up, bf16[32,256]{1,0:T(8,128)(2,1)S(1)} %get-tuple-element.19.head, bf16[512,256]{1,0:T(8,128)(2,1)S(1)} %get-tuple-element.20.spread), custom_call_target="tpu_custom_call" | custom-call | tf_op jit(solution)/shard_map/pallas_call | solution.py:296
